TPU v7x, 768 devices: a whole 4x8x12 slice. The times are simulated.
768 devices in a mesh: heads: 4 (over x), team: 2 (over core), blk: 96 (over z, y).
Axes of the slice: x: 4, y: 8, z: 12, core: 2. Of those that a mesh axis runs over, the one named last changes fastest.
Arguments:
- queries: bfloat16 [4, 3072, 32, 128], P('heads', ('team', 'blk')), may hold values from -26 to 26
- keys: bfloat16 [4, 3072, 8, 128], P('heads', ('team', 'blk')), may hold values from -26 to 26
- values: bfloat16 [4, 3072, 8, 128], P('heads', ('team', 'blk')), may hold values from -6 to 6
- run_index: int32 [192], replicated, may hold values from 0 to 191, each once
Outputs:
- attended: bfloat16 [12288, 32, 128], P(('team', 'blk'), 'heads')
All inputs are finite; a program needn't handle non-finite values.
Results may differ from a plain program's by a relative error of at most 0.012.
The roundings to bfloat16 on the way count: a program that leaves them out, or rounds other values in their place, can miss the bound.
Values may be sent and summed in bfloat16 or wider, within the bound.
No kernel may reach another device: no remote copies, remote signals or barrier semaphores. Data moves between devices by JAX's collectives and lax.ppermute only.
A program may use at most 32 MiB of HBM per device.

v0:
```python
import math

import jax
import jax.numpy as jnp
from jax import lax
from jax.sharding import PartitionSpec as P

mask_floor = -1e30
rope_theta = 500000.0
rope_factor = 8.0
low_factor = 1.0
high_factor = 4.0
initial_context = 8192.0


def combined_all(value, axis, join):
    pieces = jax.tree.map(lambda part: lax.all_gather(part, axis), value)
    head = jax.tree.map(lambda part: part[0], pieces)
    tail = jax.tree.map(lambda part: part[1:], pieces)
    so_far, _ = lax.scan(lambda so_far, slab: (join(so_far, slab), None), head, tail)
    return so_far


def inverse_freqs(head_width):
    half_width = head_width // 2
    counter = jnp.arange(half_width, dtype=jnp.float32)
    base_freq = 1.0 / rope_theta ** (2.0 * counter / head_width)
    wavelength = 2.0 * jnp.pi / base_freq
    smooth = (initial_context / wavelength - low_factor) / (high_factor - low_factor)
    blended = (1.0 - smooth) * base_freq / rope_factor + smooth * base_freq
    middle = jnp.where(wavelength > initial_context / low_factor, base_freq / rope_factor, blended)
    return jnp.where(wavelength < initial_context / high_factor, base_freq, middle)


def rotate_heads(values_in, positions, inverse):
    half_width = values_in.shape[-1] // 2
    angles = positions.astype(jnp.float32)[:, None] * inverse[None, :]
    cosine = jnp.cos(angles)[:, None, :]
    sine_part = jnp.sin(angles)[:, None, :]
    first_half = values_in[..., :half_width]
    second = values_in[..., half_width:]
    return jnp.concatenate(
        [first_half * cosine - second * sine_part, second * cosine + first_half * sine_part],
        axis=-1,
    )


def slot_positions(run_index, slot_ids, local_rows, half_rows):
    slot_count = run_index.shape[0]
    matches = slot_ids[:, None] == jnp.arange(slot_count, dtype=jnp.int32)[None, :]
    run_ids = jnp.sum(jnp.where(matches, run_index[None, :], 0), axis=1)
    early_at = run_ids * half_rows + local_rows
    late_at = (2 * slot_count - 1 - run_ids) * half_rows + local_rows - half_rows
    return jnp.where(local_rows < half_rows, early_at, late_at)


def attend_update(carried, query_block, query_pos, key_block, value_block, key_pos):
    out_sum, run_max, run_total = carried
    scaling = query_block.shape[-1] ** (-0.5)
    scores = (
        jnp.einsum("qhgd,khd->qhgk", query_block, key_block, preferred_element_type=jnp.float32)
        * scaling
    )
    visible = (key_pos[None, :] <= query_pos[:, None])[:, None, None, :]
    scores = jnp.where(visible, scores, mask_floor)
    new_max = jnp.maximum(run_max, jnp.max(scores, axis=-1))
    weights = jnp.where(visible, jnp.exp(scores - new_max[..., None]), 0.0)
    factor = jnp.exp(run_max - new_max)
    new_total = run_total * factor + jnp.sum(weights, axis=-1)
    update = jnp.einsum(
        "qhgk,khd->qhgd",
        weights.astype(jnp.bfloat16),
        value_block,
        preferred_element_type=jnp.float32,
    )
    return (out_sum * factor[..., None] + update, new_max, new_total)


def combine_partials(left_part, right_part):
    sums_left, max_left, totals_left = left_part
    sums_right, max_right, totals_right = right_part
    highest = jnp.maximum(max_left, max_right)
    weight_left = jnp.exp(max_left - highest)
    weight_right = jnp.exp(max_right - highest)
    merged = sums_left * weight_left[..., None] + sums_right * weight_right[..., None]
    return (merged, highest, totals_left * weight_left + totals_right * weight_right)


def per_device(queries, keys, values, run_index):
    head_q, head_k, head_v = (
        lax.all_to_all(queries, "heads", split_axis=2, concat_axis=0, tiled=True),
        lax.all_to_all(keys, "heads", split_axis=2, concat_axis=0, tiled=True),
        lax.all_to_all(values, "heads", split_axis=2, concat_axis=0, tiled=True),
    )
    splits, piece_rows, q_local, head_width = head_q.shape
    kv_local = head_k.shape[2]
    group_size = q_local // kv_local
    row_count = splits * piece_rows
    half_rows = row_count // 2
    team_size = lax.axis_size("team")
    block_count = lax.axis_size("blk")
    team_at = lax.axis_index("team")
    block_at = lax.axis_index("blk")
    inverse = inverse_freqs(head_width)
    local_rows = jnp.arange(row_count, dtype=jnp.int32)
    own_slot = jnp.zeros((row_count,), jnp.int32) + team_at * block_count + block_at
    own_pos = slot_positions(run_index, own_slot, local_rows, half_rows)
    rot_q = rotate_heads(
        head_q.reshape(row_count, q_local, head_width).astype(jnp.float32), own_pos, inverse
    ).astype(jnp.bfloat16)
    rot_k = rotate_heads(
        head_k.reshape(row_count, kv_local, head_width).astype(jnp.float32), own_pos, inverse
    ).astype(jnp.bfloat16)
    local_v = head_v.reshape(row_count, kv_local, head_width)
    shared_q = lax.all_gather(rot_q, "team", axis=0, tiled=True)
    gathered_rows = jnp.arange(team_size * row_count, dtype=jnp.int32)
    query_slot = gathered_rows // row_count * block_count + block_at
    query_pos = slot_positions(run_index, query_slot, gathered_rows % row_count, half_rows).reshape(
        team_size, 2, half_rows
    )
    split_q = shared_q.reshape(team_size, 2, half_rows, kv_local, group_size, head_width)
    count_q = team_size * half_rows
    early_q = split_q[:, 0].reshape(count_q, kv_local, group_size, head_width)
    late_q = split_q[:, 1].reshape(count_q, kv_local, group_size, head_width)
    early_pos = query_pos[:, 0].reshape(count_q)
    late_pos = query_pos[:, 1].reshape(count_q)

    def empty_state():
        return (
            jnp.zeros((count_q, kv_local, group_size, head_width), jnp.float32),
            jnp.full((count_q, kv_local, group_size), mask_floor, jnp.float32),
            jnp.zeros((count_q, kv_local, group_size), jnp.float32),
        )

    key_piece = lax.all_gather(rot_k, "blk", axis=0, tiled=True)
    value_piece = lax.all_gather(local_v, "blk", axis=0, tiled=True)
    piece_count = key_piece.shape[0]
    shard_count = piece_count // row_count
    per_step = math.gcd(shard_count, max(1, 1536 // row_count))
    step_count = shard_count // per_step
    key_rows = jnp.arange(piece_count, dtype=jnp.int32)
    key_slot = team_at * block_count + key_rows // row_count
    key_pos = slot_positions(run_index, key_slot, key_rows % row_count, half_rows)
    key_steps = key_piece.reshape(step_count, per_step, row_count, kv_local, head_width)
    value_steps = value_piece.reshape(step_count, per_step, row_count, kv_local, head_width)
    pos_steps = key_pos.reshape(step_count, per_step, row_count)

    def one_step(carried, inputs):
        early_state, late_state = carried
        key_block, value_block, pos_block = inputs
        early_state = attend_update(
            early_state,
            early_q,
            early_pos,
            key_block[:, :half_rows].reshape(per_step * half_rows, kv_local, head_width),
            value_block[:, :half_rows].reshape(per_step * half_rows, kv_local, head_width),
            pos_block[:, :half_rows].reshape(per_step * half_rows),
        )
        late_state = attend_update(
            late_state,
            late_q,
            late_pos,
            key_block.reshape(per_step * row_count, kv_local, head_width),
            value_block.reshape(per_step * row_count, kv_local, head_width),
            pos_block.reshape(per_step * row_count),
        )
        return ((early_state, late_state), None)

    result, unused = lax.scan(
        one_step, (empty_state(), empty_state()), (key_steps, value_steps, pos_steps)
    )
    early_state, late_state = result

    def joined(early_part, late_part):
        trailing = early_part.shape[1:]
        stacked = jnp.concatenate(
            [
                early_part.reshape((team_size, half_rows) + trailing),
                late_part.reshape((team_size, half_rows) + trailing),
            ],
            axis=1,
        )
        return stacked.reshape((team_size, row_count, q_local) + early_part.shape[3:])

    out_sum = joined(early_state[0], late_state[0])
    run_max = joined(early_state[1], late_state[1])
    run_total = joined(early_state[2], late_state[2])
    merged, highest, totals_all = combined_all(
        (out_sum, run_max, run_total), "team", combine_partials
    )
    own_sum = lax.dynamic_index_in_dim(merged, team_at, 0, keepdims=False)
    own_total = lax.dynamic_index_in_dim(totals_all, team_at, 0, keepdims=False)
    return (own_sum / own_total[..., None]).astype(jnp.bfloat16)


def solution(mesh):
    in_specs = (
        P("heads", ("team", "blk"), None, None),
        P("heads", ("team", "blk"), None, None),
        P("heads", ("team", "blk"), None, None),
        P(),
    )
    out_specs = P(("team", "blk"), "heads", None)
    return jax.shard_map(
        per_device, mesh=mesh, in_specs=in_specs, out_specs=out_specs, check_vma=False
    )
```

profile of v0, /device:TPU:1, one launch (start us, length us, event | category | flops | bytes accessed | tf_op | source)
XLA Modules:
  0.0 345.2 jit_solution(16751884919795522739)
XLA Ops:
  6.5 1.4 copy.74
  7.9 4.8 %all-to-all-start = ((bf16[1,16,8,128]{3,1,0,2:T(8,128)(2,1)}), bf16[1,16,8,128]{3,1,0,2:T(8,128)(2,1)S(1)}, u32[]{:S(2)}, u32[]{:S(2)}) async-start(bf16[1,16,8,128]{3,1,0,2:T(8,128)(2,1)} %copy.74), calls=%async_computation | async-start | bytes 65536 | tf_op jit(solution)/shard_map/all_to_all | solution.py:92
  13.8 3.2 all-to-all-done
  18.7 6.6 %all_to_all.33 = bf16[1,16,8,128]{3,1,0,2:T(8,128)(2,1)S(1)} all-to-all(bf16[1,16,8,128]{3,1,0,2:T(8,128)(2,1)S(1)} %copy.81), channel_id=1, replica_groups=mesh['heads'=4,'team'=2,'blk'=96] {'heads'}, dimensions={2} | all-to-all | bytes 65536 | tf_op jit(solution)/shard_map/all_to_all | solution.py:93
  26.0 1.6 copy.77
  27.6 3.3 all-to-all-start.1
  31.0 1.5 select_reduce_fusion
  33.9 1.9 all-to-all-done.1
  36.1 14.0 %all_gather.19 = bf16[128,8,128]{2,1,0:T(8,128)(2,1)S(1)} all-gather(bf16[64,8,128]{2,1,0:T(8,128)(2,1)S(1)} %pad_maximum_fusion.1), channel_id=1, replica_groups=mesh['heads'=4,'team'=2,'blk'=96] {'team'}, dimensions={0}, use_global_device_ids=true | all-gather | bytes 393216 | tf_op jit(solution)/shard_map/all_gather | solution.py:115
  50.8 91.4 %all-gather.4.cloned.1.call-done = bf16[6144,2,128]{2,0,1:T(8,128)(2,1)} async-done(((bf16[64,2,128]{2,0,1:T(8,128)(2,1)}), bf16[6144,2,128]{2,0,1:T(8,128)(2,1)}) %all-gather.4.cloned.1.call-update) | async-done | bytes 3145744 | tf_op jit(solution)/shard_map/all_gather | solution.py:135
  142.2 124.8 %all-gather.6.cloned.1.call-done = bf16[6144,2,128]{2,0,1:T(8,128)(2,1)} async-done(((bf16[64,2,128]{2,0,1:T(8,128)(2,1)}), bf16[6144,2,128]{2,0,1:T(8,128)(2,1)}) %all-gather.6.cloned.1.call-update) | async-done | bytes 3145744 | tf_op jit(solution)/shard_map/all_gather | solution.py:136
  267.0 41.4 %while.7 = (s32[]{:T(128)}, f32[64,2,4,128]{3,0,2,1:T(8,128)S(1)}, f32[64,2,4]{0,2,1:T(4,128)S(1)}, f32[64,2,4]{0,2,1:T(4,128)S(1)}, f32[64,2,4,128]{3,0,2,1:T(8...) while((s32[]{:T(128)}, f32[64,2,4,128]{3,0,2,1:T(8,128)S(1)}, ...), condition=%wide.wide.region_8.9_spmd.clone, body=%wide.wide.region_3.8_spmd.clone.sunk | while | flops 615142400 | bytes 41275216 | solution.py:169
  267.8 1.2 constant_dynamic-slice_fusion.11
  269.0 1.6 fusion.104
  272.3 1.3 fusion.101
  273.7 1.4 fusion.103
  278.1 1.2 constant_dynamic-slice_fusion.11
  279.3 1.7 fusion.104
  282.7 1.3 fusion.101
  284.0 1.4 fusion.103
  288.5 1.2 constant_dynamic-slice_fusion.11
  289.7 1.7 fusion.104
  293.0 1.3 fusion.101
  294.4 1.4 fusion.103
  298.8 1.2 constant_dynamic-slice_fusion.11
  300.0 1.7 fusion.104
  303.4 1.3 fusion.101
  304.7 1.4 fusion.103
  311.1 8.8 %all_gather.22 = f32[2,2,64,8]{2,3,1,0:T(8,128)S(1)} all-gather(f32[1,2,64,8]{2,3,1,0:T(8,128)S(1)} %copy.89), channel_id=1, replica_groups=mesh['heads'=4,'team'=2,'blk'=96] {'team'}, dimensions={0}, use_global_device_ids=true | all-gather | bytes 12288 | tf_op jit(solution)/shard_map/all_gather | solution.py:17
  320.2 1.8 all_gather.23
  322.1 14.4 %all-gather.8.cloned.1.call-done = f32[2,2,64,8,128]{4,3,2,1,0:T(8,128)} async-done(((f32[1,2,64,8,128]{4,3,2,1,0:T(8,128)}), f32[2,2,64,8,128]{4,3,2,1,0:T(8,128)}) %all-gather.8.cloned.1.call-update) | async-done | bytes 1048592 | tf_op jit(solution)/shard_map/all_gather | solution.py:17
  336.5 1.3 slice_bitcast_fusion.1
  (182 shorter events, 28.1 us)
Async XLA Ops:
  7.9 9.1 %all-to-all-start = ((bf16[1,16,8,128]{3,1,0,2:T(8,128)(2,1)}), bf16[1,16,8,128]{3,1,0,2:T(8,128)(2,1)S(1)}, u32[]{:S(2)}, u32[]{:S(2)}) async-start(bf16[1,16,8,128]{3,1,0,2:T(8,128)(2,1)} %copy.74), calls=%async_computation | async-start | bytes 65536 | tf_op jit(solution)/shard_map/all_to_all | solution.py:92
  12.7 129.5 %all-gather.4.cloned.1.call-start = ((), (), s32[]{:S(2)}) async-start(), calls=%async_computation.3 | async-start | bytes 3178496 | tf_op jit(solution)/shard_map/all_gather | solution.py:135
  17.9 249.2 %all-gather.6.cloned.1.call-start = ((), (), s32[]{:S(2)}) async-start(), calls=%async_computation.4 | async-start | bytes 3178496 | tf_op jit(solution)/shard_map/all_gather | solution.py:136
  27.6 8.2 %all-to-all-start.1 = ((bf16[1,16,32,128]{3,1,0,2:T(8,128)(2,1)}), bf16[1,16,32,128]{3,1,0,2:T(8,128)(2,1)S(1)}, u32[]{:S(2)}, u32[]{:S(2)}) async-start(bf16[1,16,32,128]{3,1,0,2:T(8,128)(2,1)} %copy.77), calls=%async_computation.1 | async-start | bytes 262144 | tf_op jit(solution)/shard_map/all_to_all | solution.py:91
  30.9 305.6 %all-gather.8.cloned.1.call-start = ((), (), s32[]{:S(2)}) async-start(), calls=%async_computation.5 | async-start | bytes 1572864 | tf_op jit(solution)/shard_map/all_gather | solution.py:17
  33.7 233.4 %copy-start.5 = (s32[2,1,32]{2,1,0:T(1,128)}, s32[2,1,32]{2,1,0:T(1,128)S(1)}, u32[]{:S(2)}) copy-start(s32[2,1,32]{2,1,0:T(1,128)S(1)} %get-tuple-element.290) | copy-start | bytes 772
  33.7 233.4 %copy-start.6 = (s32[2,1,32]{2,1,0:T(1,128)}, s32[2,1,32]{2,1,0:T(1,128)S(1)}, u32[]{:S(2)}) copy-start(s32[2,1,32]{2,1,0:T(1,128)S(1)} %get-tuple-element.291) | copy-start | bytes 772
  267.0 0.6 copy-start.1
  272.2 3.4 copy-start
  273.7 2.0 copy-start.3
  276.5 0.7 copy-start.4
  276.5 0.8 copy-start.2
  277.4 0.6 copy-start.1
  282.6 3.4 copy-start
  284.0 2.0 copy-start.3
  286.9 0.7 copy-start.4
  286.9 0.8 copy-start.2
  287.7 0.6 copy-start.1
  292.9 3.4 copy-start
  294.4 2.0 copy-start.3
  297.2 0.7 copy-start.4
  297.2 0.8 copy-start.2
  298.1 0.6 copy-start.1
  303.2 3.4 copy-start
  304.7 2.0 copy-start.3
  307.6 0.7 copy-start.4
  307.6 0.8 copy-start.2
Sparse Core Ops, SparseCore 0:
  18.0 124.1 all-gather.3
  146.0 121.0 all-gather.5
  310.8 25.6 all-gather.7
where the time goes:
time: 347 us; the launch traced here: 345 us
  waiting for transfers between devices  236 us (68%)
  blocking collectives  31.2 us (9%)
  local copies, waits for them, and re-layouts  26.1 us (8%)
  matrix products  17.7 us (5%)
  between operations  13.3 us (4%)
  other arithmetic  12.3 us (4%)
  starting transfers between devices  8.24 us (2%)
    all_gather x1, waiting for transfers between devices, per_device(): value_piece = lax.all_gather(local_v, 'blk', axis=0, tiled=True)  125 us
    all_gather x1, waiting for transfers between devices, per_device(): key_piece = lax.all_gather(rot_k, 'blk', axis=0, tiled=True)  91.4 us
    all_gather x1, waiting for transfers between devices, combined_all(): pieces = jax.tree.map(lambda part: lax.all_gather(part, axis), value)  14.4 us
    all_gather x1, blocking collectives, per_device(): shared_q = lax.all_gather(rot_q, 'team', axis=0, tiled=True)  14 us
    dot_general x8, matrix products, attend_update(): jnp.einsum('qhgd,khd->qhgk', query_block, key_block, preferred_element_ty...  12.2 us
    all_gather x2, blocking collectives, combined_all(): pieces = jax.tree.map(lambda part: lax.all_gather(part, axis), value)  10.6 us
    squeeze x12, local copies, waits for them, and re-layouts, per_device(): lax.scan(one_step, (empty_state(), empty_state()), (key_steps, value_step...  8.48 us
  transfers between devices with their start and end apart: 5, of which 5 were waited for; matrix products, arithmetic and copies ran while one was open for 3% of the time, Pallas kernels for 0%

commit v1 on v0

v1 whole, which is shorter than its diff:
```python
import math

import jax
import jax.numpy as jnp
from jax import lax
from jax.experimental import pallas as pl
from jax.experimental.pallas import tpu as pltpu
from jax.sharding import Mesh, PartitionSpec as P

mask_floor = -1e30
rope_theta = 500000.0
rope_factor = 8.0
low_factor = 1.0
high_factor = 4.0
initial_context = 8192.0

X, T, Z, Y = 4, 2, 12, 8
PIECE = 16
HALF = 32
GROUP = 4
HD = 128
SLOTS = T * Z * Y
Q_ROWS = GROUP * PIECE
KEYS = Z * T * 2 * PIECE
LANES = 2 * Q_ROWS
MSG = 2 * HD + 16
LOG2_SCALE = HD ** -0.5 * math.log2(math.e)


def inverse_freqs(head_width):
    half_width = head_width // 2
    counter = jnp.arange(half_width, dtype=jnp.float32)
    base_freq = 1.0 / rope_theta ** (2.0 * counter / head_width)
    wavelength = 2.0 * jnp.pi / base_freq
    smooth = (initial_context / wavelength - low_factor) / (high_factor - low_factor)
    blended = (1.0 - smooth) * base_freq / rope_factor + smooth * base_freq
    middle = jnp.where(wavelength > initial_context / low_factor, base_freq / rope_factor, blended)
    return jnp.where(wavelength < initial_context / high_factor, base_freq, middle)


def rotate(x, cosine, sine):
    half = HD // 2
    first, second = x[..., :half], x[..., half:]
    return jnp.concatenate(
        [first * cosine - second * sine, second * cosine + first * sine], axis=-1
    ).astype(jnp.bfloat16)


def attend_kernel(q_run, k_run, q_ref, kv_ref, o_ref, k_s, vt_s, kpos_s):
    bf, f32 = jnp.bfloat16, jnp.float32
    for half in range(2):
        picked = kv_ref[:, 2 * half : 2 * half + 2]
        rows = slice(half * KEYS, (half + 1) * KEYS)
        k_s[rows, :] = picked[:, :, :, 0].reshape(KEYS, HD)
        vt_s[:, rows] = picked[:, :, :, 1].reshape(KEYS, HD).T
    row = lax.broadcasted_iota(jnp.int32, (PIECE, HD), 0)
    for z in range(Z):
        for x in range(4):
            for t in range(T):
                run = k_run[t * Z + z]
                base = run * HALF if x < 2 else (2 * SLOTS - 1 - run) * HALF
                at = (x // 2) * KEYS + ((z * 2 + x % 2) * T + t) * PIECE
                kpos_s[at : at + PIECE, :] = row + (base + (x % 2) * PIECE)
    lane = lax.broadcasted_iota(jnp.int32, (1, LANES), 1)
    local = (lane // Q_ROWS) * PIECE + lane % PIECE

    def softmax_part(q_tile, q_pos, n_keys, n_free):
        s = lax.dot_general(
            k_s[:n_keys, :], q_tile, (((1,), (1,)), ((), ())), preferred_element_type=f32
        )
        kp = kpos_s[n_free:n_keys, :]
        visible = jnp.concatenate([kp, kp], axis=1) <= q_pos
        tail = jnp.where(visible, s[n_free:], mask_floor)
        s = jnp.concatenate([s[:n_free], tail], axis=0) if n_free else tail
        top = jnp.max(s, axis=0, keepdims=True)
        w = jnp.exp2((s - top) * LOG2_SCALE)
        total = jnp.sum(w, axis=0, keepdims=True)
        o = lax.dot_general(
            vt_s[:, :n_keys], w.astype(bf), (((1,), (0,)), ((), ())), preferred_element_type=f32
        )
        lse = top * LOG2_SCALE + jnp.log2(total)
        hi = lse.astype(bf).astype(f32)
        mid = (lse - hi).astype(bf).astype(f32)
        low = lse - hi - mid
        return (o * (1.0 / total)).astype(bf), [hi, mid, low]

    def step(y, carry):
        def tile(x0):
            return jnp.concatenate(
                [q_ref[y, x0 + x, t] for t in range(T) for x in range(2)], axis=0
            )

        runs = [q_run[t * Y + y] for t in range(T)]
        pos_e = jnp.concatenate([local + r * HALF for r in runs], axis=1)
        pos_l = jnp.concatenate([local + (2 * SLOTS - 1 - r) * HALF for r in runs], axis=1)
        o_e, st_e = softmax_part(tile(0), pos_e, KEYS, 0)
        o_l, st_l = softmax_part(tile(2), pos_l, 2 * KEYS, KEYS)
        pad = jnp.zeros((10, LANES), f32)
        for t in range(T):
            cols = slice(t * LANES, (t + 1) * LANES)
            o_ref[t, y, :HD, :] = o_e[:, cols]
            o_ref[t, y, HD : 2 * HD, :] = o_l[:, cols]
            stats = jnp.concatenate([v[:, cols] for v in st_e + st_l] + [pad], axis=0)
            o_ref[t, y, 2 * HD :, :] = stats.astype(bf)
        return carry

    lax.fori_loop(0, Y, step, 0)


def combine_kernel(r_ref, o_ref):
    f32 = jnp.float32
    for half in range(2):
        heads = []
        for t in range(T):
            lse = []
            for y in range(Y):
                st = r_ref[t, y, 2 * HD :, :].astype(f32)
                at = 3 * half
                lse.append(st[at : at + 1] + st[at + 1 : at + 2] + st[at + 2 : at + 3])
            top = lse[0]
            for v in lse[1:]:
                top = jnp.maximum(top, v)
            ws = [jnp.exp2(v - top) for v in lse]
            total = ws[0]
            for v in ws[1:]:
                total = total + v
            acc = jnp.zeros((HD, LANES), f32)
            for y in range(Y):
                acc = acc + r_ref[t, y, half * HD : (half + 1) * HD, :].astype(f32) * ws[y]
            heads.append((acc * (1.0 / total)).T)
        for p in range(2):
            for t in range(T):
                for j in range(GROUP):
                    at = p * Q_ROWS + j * PIECE
                    rows = slice(half * HALF + p * PIECE, half * HALF + (p + 1) * PIECE)
                    o_ref[t * GROUP + j, rows, :] = heads[t][at : at + PIECE].astype(jnp.bfloat16)


def per_device(queries, keys, values, run_index):
    bf, f32 = jnp.bfloat16, jnp.float32
    x_at, t_at = lax.axis_index("heads"), lax.axis_index("team")
    z_at, y_at = lax.axis_index("z"), lax.axis_index("y")
    runs = run_index.reshape(T, Z, Y)
    own_run = lax.dynamic_index_in_dim(run_index, (t_at * Z + z_at) * Y + y_at, 0)
    local = x_at * PIECE + jnp.arange(PIECE, dtype=jnp.int32)
    early_at = own_run * HALF + local
    late_at = (2 * SLOTS - 1 - own_run) * HALF + local - HALF
    pos = jnp.where(local < HALF, early_at, late_at)
    angles = pos.astype(f32)[:, None] * inverse_freqs(HD)[None, :]
    cosine, sine = jnp.cos(angles)[:, None, :], jnp.sin(angles)[:, None, :]
    rot_q = rotate(queries[0].astype(f32), cosine, sine)
    rot_k = rotate(keys[0].astype(f32), cosine, sine)
    n_g = keys.shape[2]
    packed = jnp.concatenate(
        [rot_q.reshape(PIECE, n_g, GROUP, HD), rot_k[:, :, None], values[0][:, :, None]], axis=2
    )
    packed = packed.transpose(1, 2, 0, 3).reshape(n_g, (GROUP + 2) * PIECE, HD)
    mine = lax.all_to_all(packed, ("heads", "team"), split_axis=0, concat_axis=0, tiled=True)
    q_own = mine[:, :Q_ROWS].reshape(1, X * T * Q_ROWS, HD)
    kv_own = mine[:, Q_ROWS:].reshape(X * T * 2 * PIECE, HD)
    q_all = lax.all_to_all(
        jnp.broadcast_to(q_own, (Y,) + q_own.shape[1:]), "y", split_axis=0, concat_axis=0, tiled=True
    )
    kv_all = lax.all_gather(kv_own, "z", axis=0, tiled=False)
    q_run = lax.dynamic_index_in_dim(runs, z_at, 1, keepdims=False).reshape(T * Y)
    k_run = lax.dynamic_index_in_dim(runs, y_at, 2, keepdims=False).reshape(T * Z)
    smem = pl.BlockSpec(memory_space=pltpu.SMEM)
    vmem = pl.BlockSpec(memory_space=pltpu.VMEM)
    partial = pl.pallas_call(
        attend_kernel,
        out_shape=jax.ShapeDtypeStruct((T, Y, MSG, LANES), bf),
        in_specs=[smem, smem, vmem, vmem],
        out_specs=vmem,
        scratch_shapes=[
            pltpu.VMEM((2 * KEYS, HD), bf),
            pltpu.VMEM((HD, 2 * KEYS), bf),
            pltpu.VMEM((2 * KEYS, HD), jnp.int32),
        ],
        name="attend",
    )(
        q_run,
        k_run,
        q_all.reshape(Y, X, T, Q_ROWS, HD),
        kv_all.reshape(Z, X, T, 2, PIECE, HD),
    )
    parts = lax.all_to_all(
        partial.reshape(T * Y, MSG, LANES), ("team", "y"), split_axis=0, concat_axis=0, tiled=True
    )
    out = pl.pallas_call(
        combine_kernel,
        out_shape=jax.ShapeDtypeStruct((T * GROUP, 2 * HALF, HD), bf),
        in_specs=[vmem],
        out_specs=vmem,
        name="combine",
    )(parts.reshape(T, Y, MSG, LANES))
    return out.transpose(1, 0, 2)


def solution(mesh):
    split = Mesh(mesh.devices.reshape(X, T, Z, Y), ("heads", "team", "z", "y"))
    spec = P("heads", ("team", "z", "y"), None, None)
    return jax.shard_map(
        per_device,
        mesh=split,
        in_specs=(spec, spec, spec, P()),
        out_specs=P(("team", "z", "y"), "heads", None),
        check_vma=False,
    )
```

time: 347 us -> 124 us (0.36)
  waiting for transfers between devices: 236 us -> 0.01 us
  blocking collectives: 31.2 us -> 91.7 us
  local copies, waits for them, and re-layouts: 26.1 us -> 7.4 us
  matrix products: 17.7 us -> 0 us
  Pallas kernels: 0 us -> 17.3 us
  between operations: 13.3 us -> 1.4 us
  other arithmetic: 12.3 us -> 2.19 us
  starting transfers between devices: 8.24 us -> 3.69 us
    all_gather x3 -> x0, waiting for transfers between devices: 231 us -> none  [the longest x1 125 us: per_device(): value_piece = lax.all_gather(local_v, 'blk', axis=0, tiled=True)]
    all_to_all x1 -> x2, blocking collectives: 6.64 us -> 61.3 us  [the longest x1 42.6 us: per_device(): lax.all_to_all(partial.reshape(T * Y, MSG, LANES), ('team', 'y'), split_a...]
    dot_general x16 -> x0, matrix products: 17.7 us -> none  [the longest x8 12.2 us: attend_update(): jnp.einsum('qhgd,khd->qhgk', query_block, key_block, preferred_element_ty...]
    pallas_call x0 -> x2, Pallas kernels: none -> 17.3 us  [the longest x1 15.1 us: per_device(): pl.pallas_call(attend_kernel, out_shape=jax.ShapeDtypeStruct((T, Y, MSG,...]
    squeeze x14 -> x0, local copies, waits for them, and re-layouts: 9.75 us -> none  [the longest x12 8.48 us: per_device(): lax.scan(one_step, (empty_state(), empty_state()), (key_steps, value_step...]
    reduce_sum x11 -> x0, other arithmetic: 7.89 us -> none  [the longest x8 4.86 us: attend_update(): new_total = run_total * factor + jnp.sum(weights, axis=-1)]
    all_gather x3 -> x1, blocking collectives: 24.6 us -> 30.4 us  [per_device(): kv_all = lax.all_gather(kv_own, 'z', axis=0, tiled=False)]
    all_to_all x2 -> x1, waiting for transfers between devices: 5.11 us -> 0.01 us  [per_device(): lax.all_to_all(jnp.broadcast_to(q_own, (Y,) + q_own.shape[1:]), 'y', spli...]
  transfers between devices with their start and end apart: 5 -> 1, of which waited for: 5 -> 0; matrix products, arithmetic and copies ran while one was open for 3% -> 1% of each run, Pallas kernels for 0% -> 0%
where the time goes in v1:
time: 124 us
  blocking collectives  91.7 us (74%)
  Pallas kernels  17.3 us (14%)
  local copies, waits for them, and re-layouts  7.4 us (6%)
  starting transfers between devices  3.69 us (3%)
  other arithmetic  2.19 us (2%)
  between operations  1.4 us (1%)
    all_to_all x1, blocking collectives, per_device(): lax.all_to_all(partial.reshape(T * Y, MSG, LANES), ('team', 'y'), split_a...  42.6 us
    all_gather x1, blocking collectives, per_device(): kv_all = lax.all_gather(kv_own, 'z', axis=0, tiled=False)  30.4 us
    all_to_all x1, blocking collectives, per_device(): lax.all_to_all(packed, ('heads', 'team'), split_axis=0, concat_axis=0, ti...  18.7 us
    pallas_call x1, Pallas kernels, per_device(): pl.pallas_call(attend_kernel, out_shape=jax.ShapeDtypeStruct((T, Y, MSG,...  15.1 us
    all_to_all x1, starting transfers between devices, per_device(): lax.all_to_all(jnp.broadcast_to(q_own, (Y,) + q_own.shape[1:]), 'y', spli...  3.69 us
  transfers between devices with their start and end apart: 1, of which 0 were waited for; matrix products, arithmetic and copies ran while one was open for 1% of the time, Pallas kernels for 0%

profile of v1, /device:TPU:1, one launch (start us, length us, event | category | flops | bytes accessed | tf_op | source)
XLA Modules:
  0.0 123.7 jit_solution(7887578651799622461)
XLA Ops:
  0.0 1.3 %dynamic_slice.14 = s32[1]{0:T(128)} dynamic-slice(s32[192]{0:T(256)} %param.7, s32[]{:T(128)S(6)} %select_n.37), dynamic_slice_sizes={1} | dynamic-slice | bytes 12 | tf_op jit(solution)/shard_map/jit(dynamic_index_in_dim)/dynamic_slice | solution.py:144
  2.6 0.8 copy.29
  3.4 0.8 bitcast_convert_fusion.1
  4.1 0.9 bitcast_convert_fusion
  5.1 0.1 multiply_cosine_fusion
  5.2 0.1 fusion
  5.3 0.1 subtract_convert_fusion
  5.5 0.1 copy.21
  5.5 0.1 copy.22
  5.6 0.1 pad_maximum_fusion
  5.7 18.7 %all_to_all.15 = bf16[8,96,128]{2,1,0:T(8,128)(2,1)S(1)} all-to-all(bf16[8,96,128]{2,1,0:T(8,128)(2,1)S(1)} %bitcast.33), channel_id=1, replica_groups=mesh['heads'=4,'team'=2,'z'=12,'y'=8] {'heads','team'}, dimensions={0} | all-to-all | bytes 393216 | tf_op jit(solution)/shard_map/all_to_all | solution.py:158
  24.4 1.1 broadcast_in_dim.5
  25.6 0.0 copy-start.1
  25.6 3.7 %all-to-all-start.1 = ((bf16[8,512,128]{2,1,0:T(8,128)(2,1)}), bf16[8,512,128]{2,1,0:T(8,128)(2,1)S(1)}, u32[]{:S(2)}, u32[]{:S(2)}) async-start(bf16[8,512,128]{2,1,0:T(8,128)(2,1)} %broadcast_in_dim.5), calls=%async_computation.1 | async-start | bytes 2097152 | tf_op jit(solution)/shard_map/all_to_all | solution.py:161
  29.3 0.0 copy-done.1
  29.3 0.1 reshape.147
  29.4 0.6 reshape.148.q_run
  30.0 0.2 dynamic-slice_reduce_fusion
  30.2 0.6 reshape.149.k_run
  30.7 30.4 %all_gather.3 = bf16[12,256,128]{2,1,0:T(8,128)(2,1)} all-gather(bf16[1,256,128]{2,1,0:T(8,128)(2,1)S(1)} %bitcast.38), channel_id=1, replica_groups=mesh['heads'=4,'team'=2,'z'=12,'y'=8] {'z'}, dimensions={0}, use_global_device_ids=true | all-gather | bytes 851968 | tf_op jit(solution)/shard_map/all_gather | solution.py:164
  61.1 0.0 all-to-all-done.1
  61.1 0.0 copy-start
  61.1 1.0 copy-done
  62.2 15.1 %attend.1 = bf16[2,8,272,128]{3,2,1,0:T(8,128)(2,1)} custom-call(s32[16]{0:T(128)} %reshape.148.q_run, s32[24]{0:T(128)} %reshape.149.k_run, bf16[8,4,2,64,128]{4,3,2,1,0:T(8,128)(2,1)} %bitcast.31, bf16[12,4,2,2,16,128]{5,4,3,2,1,0:T(8,128)(2,1)} %bitcast.32), custom_call_target="tpu_custom_call" | custom-call | tf_op jit(solution)/shard_map/attend/pallas_call | solution.py:169
  77.3 42.6 %all_to_all.16 = bf16[16,272,128]{2,1,0:T(8,128)(2,1)} all-to-all(bf16[16,272,128]{2,1,0:T(8,128)(2,1)} %bitcast.30), channel_id=1, replica_groups=mesh['heads'=4,'team'=2,'z'=12,'y'=8] {'team','y'}, dimensions={0} | all-to-all | bytes 2228224 | tf_op jit(solution)/shard_map/all_to_all | solution.py:186
  119.9 2.2 %combine.1 = bf16[8,64,128]{2,1,0:T(8,128)(2,1)} custom-call(bf16[2,8,272,128]{3,2,1,0:T(8,128)(2,1)} %bitcast.29), custom_call_target="tpu_custom_call" | custom-call | tf_op jit(solution)/shard_map/combine/pallas_call | solution.py:189
  122.1 1.6 %copy.26 = bf16[64,8,128]{2,1,0:T(8,128)(2,1)} copy(bf16[64,8,128]{2,0,1:T(8,128)(2,1)} %bitcast.36) | data formatting | bytes 262144 | tf_op jit(solution)/shard_map/transpose | solution.py:196
  (5 shorter events, 0.1 us)
Async XLA Ops:
  25.6 3.7 %copy-start.1 = (s32[192]{0:T(256)S(1)}, s32[192]{0:T(256)}, u32[]{:S(2)}) copy-start(s32[192]{0:T(256)} %param.7) | copy-start | bytes 2308
  25.6 35.6 %all-to-all-start.1 = ((bf16[8,512,128]{2,1,0:T(8,128)(2,1)}), bf16[8,512,128]{2,1,0:T(8,128)(2,1)S(1)}, u32[]{:S(2)}, u32[]{:S(2)}) async-start(bf16[8,512,128]{2,1,0:T(8,128)(2,1)} %broadcast_in_dim.5), calls=%async_computation.1 | async-start | bytes 2097152 | tf_op jit(solution)/shard_map/all_to_all | solution.py:161
  61.1 1.0 copy-start

commit v2 on v1

v2 whole, which is shorter than its diff:
```python
import math

import jax
import jax.numpy as jnp
from jax import lax
from jax.experimental import pallas as pl
from jax.experimental.pallas import tpu as pltpu
from jax.sharding import Mesh, PartitionSpec as P

mask_floor = -1e30
rope_theta = 500000.0
rope_factor = 8.0
low_factor = 1.0
high_factor = 4.0
initial_context = 8192.0

X, T, Z, Y = 4, 2, 12, 8
PIECE = 16
HALF = 32
GROUP = 4
HD = 128
SLOTS = T * Z * Y
Q_ROWS = GROUP * PIECE
KEYS = Z * T * 2 * PIECE
LANES = 2 * Q_ROWS
MSG = 2 * HD + 16
CHUNK = 128
PRODUCE_FIRST = 1
LOG2_SCALE = HD ** -0.5 * math.log2(math.e)


def inverse_freqs(head_width):
    half_width = head_width // 2
    counter = jnp.arange(half_width, dtype=jnp.float32)
    base_freq = 1.0 / rope_theta ** (2.0 * counter / head_width)
    wavelength = 2.0 * jnp.pi / base_freq
    smooth = (initial_context / wavelength - low_factor) / (high_factor - low_factor)
    blended = (1.0 - smooth) * base_freq / rope_factor + smooth * base_freq
    middle = jnp.where(wavelength > initial_context / low_factor, base_freq / rope_factor, blended)
    return jnp.where(wavelength < initial_context / high_factor, base_freq, middle)


def pack_kernel(run_ref, freq_ref, q_ref, k_ref, v_ref, o_ref):
    f32 = jnp.float32
    x_at, t_at = lax.axis_index("heads"), lax.axis_index("team")
    z_at, y_at = lax.axis_index("z"), lax.axis_index("y")
    run = run_ref[(t_at * Z + z_at) * Y + y_at]
    base = jnp.where(x_at < 2, run * HALF, (2 * SLOTS - 1 - run) * HALF - HALF) + x_at * PIECE
    pos = lax.broadcasted_iota(jnp.int32, (PIECE, HD), 0) + base
    angles = pos.astype(f32) * freq_ref[...]
    cosine = jnp.cos(angles)[:, None, :]
    flip = jnp.where(lax.broadcasted_iota(jnp.int32, (PIECE, HD), 1) < HD // 2, -1.0, 1.0)
    sine = (jnp.sin(angles) * flip)[:, None, :]

    def turned(ref):
        x = ref[0].astype(f32)
        y = x * cosine + jnp.roll(x, HD // 2, axis=-1) * sine
        return jnp.swapaxes(y, 0, 1).astype(jnp.bfloat16)

    n_g = k_ref.shape[2]
    q = turned(q_ref).reshape(n_g, GROUP * PIECE, HD)
    o_ref[:, :Q_ROWS, :] = q
    o_ref[:, Q_ROWS : Q_ROWS + PIECE, :] = turned(k_ref)
    v = jnp.swapaxes(v_ref[0].astype(f32), 0, 1).astype(jnp.bfloat16)
    o_ref[:, Q_ROWS + PIECE :, :] = v


def attend_kernel(q_run, k_run, q_ref, kv_ref, o_ref, k_s, vt_s, kpos_s, se_s, sl_s, w_s):
    bf, f32 = jnp.bfloat16, jnp.float32
    for half in range(2):
        picked = kv_ref[:, 2 * half : 2 * half + 2]
        rows = slice(half * KEYS, (half + 1) * KEYS)
        k_s[rows, :] = picked[:, :, :, 0].reshape(KEYS, HD)
        vt_s[:, rows] = picked[:, :, :, 1].reshape(KEYS, HD).T
    row = lax.broadcasted_iota(jnp.int32, (PIECE, HD), 0)
    for z in range(Z):
        for x in range(4):
            for t in range(T):
                run = k_run[t * Z + z]
                base = run * HALF if x < 2 else (2 * SLOTS - 1 - run) * HALF
                at = (x // 2) * KEYS + ((z * 2 + x % 2) * T + t) * PIECE
                kpos_s[at : at + PIECE, :] = row + (base + (x % 2) * PIECE)
    lane = lax.broadcasted_iota(jnp.int32, (1, LANES), 1)
    local = (lane // Q_ROWS) * PIECE + lane % PIECE

    counts = (KEYS, 2 * KEYS)
    free = (0, KEYS)

    def tile(kind, y):
        return jnp.concatenate(
            [q_ref[y, 2 * kind + x, t] for t in range(T) for x in range(2)], axis=0
        )

    def q_pos(kind, y):
        runs = [q_run[t * Y + y] for t in range(T)]
        bases = [(2 * SLOTS - 1 - r) * HALF if kind else r * HALF for r in runs]
        return jnp.concatenate([local + b for b in bases], axis=1)

    def produce(kind, y, s_ref):
        q_tile, pos, top = tile(kind, y), q_pos(kind, y), None
        for at in range(0, counts[kind], CHUNK):
            rows = slice(at, at + CHUNK)
            s = lax.dot_general(
                k_s[rows, :], q_tile, (((1,), (1,)), ((), ())), preferred_element_type=f32
            )
            if at >= free[kind]:
                kp = kpos_s[rows, :]
                s = jnp.where(jnp.concatenate([kp, kp], axis=1) <= pos, s, mask_floor)
            s_ref[rows, :] = s
            best = jnp.max(s.reshape(CHUNK // 8, 8, 2 * LANES), axis=0)
            top = best if top is None else jnp.maximum(top, best)
            yield None
        yield jnp.max(top, axis=0, keepdims=True)

    def consume(kind, y, s_ref, top):
        total = jnp.zeros((8, 2 * LANES), f32)
        for at in range(0, counts[kind], CHUNK):
            rows = slice(at, at + CHUNK)
            w = jnp.exp2((s_ref[rows, :] - top) * LOG2_SCALE)
            total = total + jnp.sum(w.reshape(CHUNK // 8, 8, 2 * LANES), axis=0)
            w_s[kind, rows, :] = w.astype(bf)
            yield None
        total = jnp.sum(total, axis=0, keepdims=True)
        n = counts[kind]
        o = lax.dot_general(
            vt_s[:, :n], w_s[kind, :n, :], (((1,), (0,)), ((), ())), preferred_element_type=f32
        )
        o = (o * (1.0 / total)).astype(bf)
        lse = top * LOG2_SCALE + jnp.log2(total)
        hi = lse.astype(bf).astype(f32)
        mid = (lse - hi).astype(bf).astype(f32)
        low = lse - hi - mid
        pad = jnp.zeros((5, 2 * LANES), f32)
        stats = jnp.concatenate([hi, mid, low, pad], axis=0).astype(bf)
        for t in range(T):
            cols = slice(t * LANES, (t + 1) * LANES)
            o_ref[t, y, kind * HD : (kind + 1) * HD, :] = o[:, cols]
            o_ref[t, y, 2 * HD + 8 * kind : 2 * HD + 8 * kind + 8, :] = stats[:, cols]
        yield None

    def together(make, use):
        top, left = None, True
        ratio = PRODUCE_FIRST
        while left:
            left = False
            for _ in range(ratio):
                for got in make:
                    left = True
                    top = got if got is not None else top
                    break
            for _ in use:
                left = True
                break
        return top

    def only(make):
        top = None
        for got in make:
            top = got if got is not None else top
        return top

    def step(y, top_e):
        top_l = together(produce(1, y, sl_s), consume(0, y, se_s, top_e))
        after = jnp.minimum(y + 1, Y - 1)
        return together(produce(0, after, se_s), consume(1, y, sl_s, top_l))

    lax.fori_loop(0, Y, step, only(produce(0, 0, se_s)))


def combine_kernel(r_ref, o_ref):
    f32 = jnp.float32
    for half in range(2):
        heads = []
        for t in range(T):
            lse = []
            for y in range(Y):
                st = r_ref[t, y, 2 * HD + 8 * half : 2 * HD + 8 * half + 8, :].astype(f32)
                at = 0
                lse.append(st[at : at + 1] + st[at + 1 : at + 2] + st[at + 2 : at + 3])
            top = lse[0]
            for v in lse[1:]:
                top = jnp.maximum(top, v)
            ws = [jnp.exp2(v - top) for v in lse]
            total = ws[0]
            for v in ws[1:]:
                total = total + v
            acc = jnp.zeros((HD, LANES), f32)
            for y in range(Y):
                acc = acc + r_ref[t, y, half * HD : (half + 1) * HD, :].astype(f32) * ws[y]
            heads.append((acc * (1.0 / total)).T)
        for p in range(2):
            block = jnp.stack(
                [
                    heads[t][p * Q_ROWS + j * PIECE : p * Q_ROWS + (j + 1) * PIECE]
                    for t in range(T)
                    for j in range(GROUP)
                ],
                axis=0,
            )
            at = half * HALF + p * PIECE
            o_ref[at : at + PIECE] = jnp.swapaxes(block, 0, 1).astype(jnp.bfloat16)


def per_device(queries, keys, values, run_index):
    bf, f32 = jnp.bfloat16, jnp.float32
    z_at, y_at = lax.axis_index("z"), lax.axis_index("y")
    runs = run_index.reshape(T, Z, Y)
    smem = pl.BlockSpec(memory_space=pltpu.SMEM)
    vmem = pl.BlockSpec(memory_space=pltpu.VMEM)
    freqs = inverse_freqs(HD)
    packed = pl.pallas_call(
        pack_kernel,
        out_shape=jax.ShapeDtypeStruct((X * T, (GROUP + 2) * PIECE, HD), bf),
        in_specs=[smem, vmem, vmem, vmem, vmem],
        out_specs=vmem,
        compiler_params=pltpu.CompilerParams(vmem_limit_bytes=8 << 20),
        name="pack",
    )(run_index, jnp.concatenate([freqs, freqs])[None, :], queries, keys, values)
    mine = lax.all_to_all(packed, ("heads", "team"), split_axis=0, concat_axis=0, tiled=True)
    q_own = mine[:, :Q_ROWS].reshape(1, X * T * Q_ROWS, HD)
    kv_own = mine[:, Q_ROWS:].reshape(X * T * 2 * PIECE, HD)
    q_all = lax.all_to_all(
        jnp.broadcast_to(q_own, (Y,) + q_own.shape[1:]), "y", split_axis=0, concat_axis=0, tiled=True
    )
    kv_all = lax.all_gather(kv_own, "z", axis=0, tiled=False)
    q_run = lax.dynamic_index_in_dim(runs, z_at, 1, keepdims=False).reshape(T * Y)
    k_run = lax.dynamic_index_in_dim(runs, y_at, 2, keepdims=False).reshape(T * Z)
    partial = pl.pallas_call(
        attend_kernel,
        out_shape=jax.ShapeDtypeStruct((T, Y, MSG, LANES), bf),
        in_specs=[smem, smem, vmem, vmem],
        out_specs=vmem,
        scratch_shapes=[
            pltpu.VMEM((2 * KEYS, HD), bf),
            pltpu.VMEM((HD, 2 * KEYS), bf),
            pltpu.VMEM((2 * KEYS, HD), jnp.int32),
            pltpu.VMEM((KEYS, 2 * LANES), f32),
            pltpu.VMEM((2 * KEYS, 2 * LANES), f32),
            pltpu.VMEM((2, 2 * KEYS, 2 * LANES), bf),
        ],
        compiler_params=pltpu.CompilerParams(vmem_limit_bytes=24 << 20),
        name="attend",
    )(
        q_run,
        k_run,
        q_all.reshape(Y, X, T, Q_ROWS, HD),
        kv_all.reshape(Z, X, T, 2, PIECE, HD),
    )
    parts = lax.all_to_all(
        partial.reshape(T * Y, MSG, LANES), ("team", "y"), split_axis=0, concat_axis=0, tiled=True
    )
    return pl.pallas_call(
        combine_kernel,
        out_shape=jax.ShapeDtypeStruct((2 * HALF, T * GROUP, HD), bf),
        in_specs=[vmem],
        out_specs=vmem,
        compiler_params=pltpu.CompilerParams(vmem_limit_bytes=8 << 20),
        name="combine",
    )(parts.reshape(T, Y, MSG, LANES))


def solution(mesh):
    split = Mesh(mesh.devices.reshape(X, T, Z, Y), ("heads", "team", "z", "y"))
    spec = P("heads", ("team", "z", "y"), None, None)
    return jax.shard_map(
        per_device,
        mesh=split,
        in_specs=(spec, spec, spec, P()),
        out_specs=P(("team", "z", "y"), "heads", None),
        check_vma=False,
    )
```

time: 124 us -> 110 us (0.89)
  Pallas kernels: 17.3 us -> 11.5 us
  local copies, waits for them, and re-layouts: 7.4 us -> 4.69 us
  other arithmetic: 2.19 us -> 0.1 us
  blocking collectives: 91.7 us -> 89.8 us
  between operations: 1.4 us -> 0.05 us
    pallas_call x1, Pallas kernels: 15.1 us -> 9.73 us  [per_device(): pl.pallas_call(attend_kernel, out_shape=jax.ShapeDtypeStruct((T, Y, MSG,...]
    convert_element_type x3 -> x0, other arithmetic: 1.7 us -> none  [the longest x1 0.92 us: per_device(): rot_q = rotate(queries[0].astype(f32), cosine, sine)]
    transpose x1 -> x0, local copies, waits for them, and re-layouts: 1.65 us -> none  [per_device(): return out.transpose(1, 0, 2)]
    unnamed x5 -> x10, local copies, waits for them, and re-layouts: 1.79 us -> 3.1 us
    all_gather x1, blocking collectives: 30.4 us -> 29.1 us  [per_device(): kv_all = lax.all_gather(kv_own, 'z', axis=0, tiled=False)]
    dynamic_slice x1 -> x0, local copies, waits for them, and re-layouts: 1.27 us -> none  [per_device(): lax.dynamic_index_in_dim(run_index, (t_at * Z + z_at) * Y + y_at, 0)]
  transfers between devices with their start and end apart: 1 -> 1, of which waited for: 0 -> 0; matrix products, arithmetic and copies ran while one was open for 1% -> 0% of each run, Pallas kernels for 0% -> 0%
where the time goes in v2:
time: 110 us
  blocking collectives  89.8 us (82%)
  Pallas kernels  11.5 us (10%)
  local copies, waits for them, and re-layouts  4.69 us (4%)
  starting transfers between devices  3.69 us (3%)
    all_to_all x1, blocking collectives, per_device(): lax.all_to_all(partial.reshape(T * Y, MSG, LANES), ('team', 'y'), split_a...  42 us
    all_gather x1, blocking collectives, per_device(): kv_all = lax.all_gather(kv_own, 'z', axis=0, tiled=False)  29.1 us
    all_to_all x1, blocking collectives, per_device(): lax.all_to_all(packed, ('heads', 'team'), split_axis=0, concat_axis=0, ti...  18.7 us
    pallas_call x1, Pallas kernels, per_device(): pl.pallas_call(attend_kernel, out_shape=jax.ShapeDtypeStruct((T, Y, MSG,...  9.73 us
    all_to_all x1, starting transfers between devices, per_device(): lax.all_to_all(jnp.broadcast_to(q_own, (Y,) + q_own.shape[1:]), 'y', spli...  3.69 us
    unnamed x10, local copies, waits for them, and re-layouts  3.1 us
  transfers between devices with their start and end apart: 1, of which 0 were waited for; matrix products, arithmetic and copies ran while one was open for 0% of the time, Pallas kernels for 0%

profile of v2, /device:TPU:1, one launch (start us, length us, event | category | flops | bytes accessed | tf_op | source)
XLA Modules:
  0.0 109.8 jit_solution(3638921941896158017)
XLA Ops:
  0.0 0.1 maximum_bitcast_fusion.freq_ref
  0.1 0.0 copy-start
  0.1 0.9 copy-done
  1.0 0.0 copy-start.1
  1.0 0.8 copy-done.1
  1.8 0.0 copy-start.2
  1.8 0.8 copy-done.2
  2.5 0.0 copy-start.3
  2.5 0.7 copy-done.3
  3.2 0.8 pack.1
  4.0 18.7 %all_to_all.15 = bf16[8,96,128]{2,1,0:T(8,128)(2,1)S(1)} all-to-all(bf16[8,96,128]{2,1,0:T(8,128)(2,1)S(1)} %pack.1), channel_id=1, replica_groups=mesh['heads'=4,'team'=2,'z'=12,'y'=8] {'heads','team'}, dimensions={0} | all-to-all | bytes 393216 | tf_op jit(solution)/shard_map/all_to_all | solution.py:219
  22.7 1.1 %broadcast_in_dim.12 = bf16[8,512,128]{2,1,0:T(8,128)(2,1)} broadcast(bf16[512,128]{1,0:T(8,128)(2,1)S(1)} %bitcast.12), dimensions={1,2} | broadcast | bytes 1179648 | tf_op jit(solution)/shard_map/broadcast_in_dim | solution.py:223
  23.8 0.0 copy-start.4
  23.8 3.7 %all-to-all-start.1 = ((bf16[8,512,128]{2,1,0:T(8,128)(2,1)}), bf16[8,512,128]{2,1,0:T(8,128)(2,1)S(1)}, u32[]{:S(2)}, u32[]{:S(2)}) async-start(bf16[8,512,128]{2,1,0:T(8,128)(2,1)} %broadcast_in_dim.12), calls=%async_computation.1 | async-start | bytes 2097152 | tf_op jit(solution)/shard_map/all_to_all | solution.py:222
  27.5 0.0 copy-done.4
  27.5 0.1 reshape.25
  27.6 0.1 reshape.26.q_run
  27.7 0.2 dynamic-slice_reduce_fusion
  27.9 0.1 reshape.27.k_run
  28.0 29.1 %all_gather.3 = bf16[12,256,128]{2,1,0:T(8,128)(2,1)S(1)} all-gather(bf16[1,256,128]{2,1,0:T(8,128)(2,1)S(1)} %bitcast.13), channel_id=1, replica_groups=mesh['heads'=4,'team'=2,'z'=12,'y'=8] {'z'}, dimensions={0}, use_global_device_ids=true | all-gather | bytes 851968 | tf_op jit(solution)/shard_map/all_gather | solution.py:225
  57.1 0.0 all-to-all-done.1
  57.1 9.7 %attend.1 = bf16[2,8,272,128]{3,2,1,0:T(8,128)(2,1)S(1)} custom-call(s32[16]{0:T(128)S(1)} %reshape.26.q_run, s32[24]{0:T(128)S(1)} %reshape.27.k_run, bf16[8,4,2,64,128]{4,3,2,1,0:T(8,128)(2,1)S(1)} %bitcast.10, bf16[12,4,2,2,16,128]{5,4,3,2,1,0:T(8,128)(2,1)S(1)} %bitcast.11), custom_call_target="tpu_custom_call" | custom-call | tf_op jit(solution)/shard_map/attend/pallas_call | solution.py:228
  66.8 42.0 %all_to_all.16 = bf16[16,272,128]{2,1,0:T(8,128)(2,1)S(1)} all-to-all(bf16[16,272,128]{2,1,0:T(8,128)(2,1)S(1)} %bitcast.9), channel_id=1, replica_groups=mesh['heads'=4,'team'=2,'z'=12,'y'=8] {'team','y'}, dimensions={0} | all-to-all | bytes 2228224 | tf_op jit(solution)/shard_map/all_to_all | solution.py:249
  108.9 1.0 combine.1
  (4 shorter events, 0.1 us)
Async XLA Ops:
  0.1 0.9 copy-start
  1.0 0.8 copy-start.1
  1.8 0.8 copy-start.2
  2.5 0.7 copy-start.3
  23.8 3.7 %copy-start.4 = (s32[192]{0:T(256)S(1)}, s32[192]{0:T(256)}, u32[]{:S(2)}) copy-start(s32[192]{0:T(256)} %run_ref.1) | copy-start | bytes 2308
  23.8 33.3 %all-to-all-start.1 = ((bf16[8,512,128]{2,1,0:T(8,128)(2,1)}), bf16[8,512,128]{2,1,0:T(8,128)(2,1)S(1)}, u32[]{:S(2)}, u32[]{:S(2)}) async-start(bf16[8,512,128]{2,1,0:T(8,128)(2,1)} %broadcast_in_dim.12), calls=%async_computation.1 | async-start | bytes 2097152 | tf_op jit(solution)/shard_map/all_to_all | solution.py:222

commit v3 on v2

--- a/solution.py
+++ b/solution.py
@@ -14,14 +14,16 @@
 high_factor = 4.0
 initial_context = 8192.0
 
-X, T, Z, Y = 4, 2, 12, 8
+X, T, Z, YH, YL = 4, 2, 12, 4, 2
+Y = YH * YL
 PIECE = 16
 HALF = 32
 GROUP = 4
 HD = 128
 SLOTS = T * Z * Y
 Q_ROWS = GROUP * PIECE
-KEYS = Z * T * 2 * PIECE
+PART = Z * YL * 2 * PIECE
+KEYS = T * PART
 LANES = 2 * Q_ROWS
 MSG = 2 * HD + 16
 CHUNK = 128
@@ -43,7 +45,7 @@
 def pack_kernel(run_ref, freq_ref, q_ref, k_ref, v_ref, o_ref):
     f32 = jnp.float32
     x_at, t_at = lax.axis_index("heads"), lax.axis_index("team")
-    z_at, y_at = lax.axis_index("z"), lax.axis_index("y")
+    z_at, y_at = lax.axis_index("z"), lax.axis_index("yh") * YL + lax.axis_index("yl")
     run = run_ref[(t_at * Z + z_at) * Y + y_at]
     base = jnp.where(x_at < 2, run * HALF, (2 * SLOTS - 1 - run) * HALF - HALF) + x_at * PIECE
     pos = lax.broadcasted_iota(jnp.int32, (PIECE, HD), 0) + base
@@ -65,21 +67,25 @@
     o_ref[:, Q_ROWS + PIECE :, :] = v
 
 
-def attend_kernel(q_run, k_run, q_ref, kv_ref, o_ref, k_s, vt_s, kpos_s, se_s, sl_s, w_s):
+def attend_kernel(run_ref, q_ref, near_ref, far_ref, o_ref, k_s, vt_s, kpos_s, se_s, sl_s, w_s):
     bf, f32 = jnp.bfloat16, jnp.float32
-    for half in range(2):
-        picked = kv_ref[:, 2 * half : 2 * half + 2]
-        rows = slice(half * KEYS, (half + 1) * KEYS)
-        k_s[rows, :] = picked[:, :, :, 0].reshape(KEYS, HD)
-        vt_s[:, rows] = picked[:, :, :, 1].reshape(KEYS, HD).T
+    t_at, z_at, yh_at = lax.axis_index("team"), lax.axis_index("z"), lax.axis_index("yh")
     row = lax.broadcasted_iota(jnp.int32, (PIECE, HD), 0)
-    for z in range(Z):
-        for x in range(4):
-            for t in range(T):
-                run = k_run[t * Z + z]
-                base = run * HALF if x < 2 else (2 * SLOTS - 1 - run) * HALF
-                at = (x // 2) * KEYS + ((z * 2 + x % 2) * T + t) * PIECE
-                kpos_s[at : at + PIECE, :] = row + (base + (x % 2) * PIECE)
+    for part, kv_ref in enumerate((near_ref, far_ref)):
+        team = t_at if part == 0 else 1 - t_at
+        for half in range(2):
+            picked = kv_ref[:, 2 * half : 2 * half + 2]
+            start = half * KEYS + part * PART
+            rows = slice(start, start + PART)
+            k_s[rows, :] = picked[:, :, :, 0].reshape(PART, HD)
+            vt_s[:, rows] = picked[:, :, :, 1].reshape(PART, HD).T
+            for z in range(Z):
+                for yl in range(YL):
+                    run = run_ref[((team * Z + z) * YH + yh_at) * YL + yl]
+                    base = (2 * SLOTS - 1 - run) * HALF if half else run * HALF
+                    for x in range(2):
+                        at = start + ((z * 2 + x) * YL + yl) * PIECE
+                        kpos_s[at : at + PIECE, :] = row + (base + x * PIECE)
     lane = lax.broadcasted_iota(jnp.int32, (1, LANES), 1)
     local = (lane // Q_ROWS) * PIECE + lane % PIECE
 
@@ -88,11 +94,11 @@
 
     def tile(kind, y):
         return jnp.concatenate(
-            [q_ref[y, 2 * kind + x, t] for t in range(T) for x in range(2)], axis=0
+            [q_ref[y, 2 * kind + x, t] for t in range(YL) for x in range(2)], axis=0
         )
 
     def q_pos(kind, y):
-        runs = [q_run[t * Y + y] for t in range(T)]
+        runs = [run_ref[((t_at * Z + z_at) * YH + y) * YL + t] for t in range(YL)]
         bases = [(2 * SLOTS - 1 - r) * HALF if kind else r * HALF for r in runs]
         return jnp.concatenate([local + b for b in bases], axis=1)
 
@@ -132,10 +138,10 @@
         low = lse - hi - mid
         pad = jnp.zeros((5, 2 * LANES), f32)
         stats = jnp.concatenate([hi, mid, low, pad], axis=0).astype(bf)
-        for t in range(T):
+        for t in range(YL):
             cols = slice(t * LANES, (t + 1) * LANES)
-            o_ref[t, y, kind * HD : (kind + 1) * HD, :] = o[:, cols]
-            o_ref[t, y, 2 * HD + 8 * kind : 2 * HD + 8 * kind + 8, :] = stats[:, cols]
+            o_ref[y, t, kind * HD : (kind + 1) * HD, :] = o[:, cols]
+            o_ref[y, t, 2 * HD + 8 * kind : 2 * HD + 8 * kind + 8, :] = stats[:, cols]
         yield None
 
     def together(make, use):
@@ -161,20 +167,20 @@
 
     def step(y, top_e):
         top_l = together(produce(1, y, sl_s), consume(0, y, se_s, top_e))
-        after = jnp.minimum(y + 1, Y - 1)
+        after = jnp.minimum(y + 1, YH - 1)
         return together(produce(0, after, se_s), consume(1, y, sl_s, top_l))
 
-    lax.fori_loop(0, Y, step, only(produce(0, 0, se_s)))
+    lax.fori_loop(0, YH, step, only(produce(0, 0, se_s)))
 
 
 def combine_kernel(r_ref, o_ref):
     f32 = jnp.float32
     for half in range(2):
         heads = []
-        for t in range(T):
+        for t in range(YL):
             lse = []
-            for y in range(Y):
-                st = r_ref[t, y, 2 * HD + 8 * half : 2 * HD + 8 * half + 8, :].astype(f32)
+            for y in range(YH):
+                st = r_ref[y, t, 2 * HD + 8 * half : 2 * HD + 8 * half + 8, :].astype(f32)
                 at = 0
                 lse.append(st[at : at + 1] + st[at + 1 : at + 2] + st[at + 2 : at + 3])
             top = lse[0]
@@ -185,14 +191,14 @@
             for v in ws[1:]:
                 total = total + v
             acc = jnp.zeros((HD, LANES), f32)
-            for y in range(Y):
-                acc = acc + r_ref[t, y, half * HD : (half + 1) * HD, :].astype(f32) * ws[y]
+            for y in range(YH):
+                acc = acc + r_ref[y, t, half * HD : (half + 1) * HD, :].astype(f32) * ws[y]
             heads.append((acc * (1.0 / total)).T)
         for p in range(2):
             block = jnp.stack(
                 [
                     heads[t][p * Q_ROWS + j * PIECE : p * Q_ROWS + (j + 1) * PIECE]
-                    for t in range(T)
+                    for t in range(YL)
                     for j in range(GROUP)
                 ],
                 axis=0,
@@ -203,32 +209,34 @@
 
 def per_device(queries, keys, values, run_index):
     bf, f32 = jnp.bfloat16, jnp.float32
-    z_at, y_at = lax.axis_index("z"), lax.axis_index("y")
-    runs = run_index.reshape(T, Z, Y)
     smem = pl.BlockSpec(memory_space=pltpu.SMEM)
     vmem = pl.BlockSpec(memory_space=pltpu.VMEM)
     freqs = inverse_freqs(HD)
     packed = pl.pallas_call(
         pack_kernel,
-        out_shape=jax.ShapeDtypeStruct((X * T, (GROUP + 2) * PIECE, HD), bf),
+        out_shape=jax.ShapeDtypeStruct((X * YL, (GROUP + 2) * PIECE, HD), bf),
         in_specs=[smem, vmem, vmem, vmem, vmem],
         out_specs=vmem,
         compiler_params=pltpu.CompilerParams(vmem_limit_bytes=8 << 20),
         name="pack",
     )(run_index, jnp.concatenate([freqs, freqs])[None, :], queries, keys, values)
-    mine = lax.all_to_all(packed, ("heads", "team"), split_axis=0, concat_axis=0, tiled=True)
-    q_own = mine[:, :Q_ROWS].reshape(1, X * T * Q_ROWS, HD)
-    kv_own = mine[:, Q_ROWS:].reshape(X * T * 2 * PIECE, HD)
+    mine = lax.all_to_all(packed, ("heads", "yl"), split_axis=0, concat_axis=0, tiled=True)
+    q_own = mine[:, :Q_ROWS].reshape(1, X * YL * Q_ROWS, HD)
+    kv_own = mine[:, Q_ROWS:].reshape(X * YL * 2 * PIECE, HD)
     q_all = lax.all_to_all(
-        jnp.broadcast_to(q_own, (Y,) + q_own.shape[1:]), "y", split_axis=0, concat_axis=0, tiled=True
-    )
-    kv_all = lax.all_gather(kv_own, "z", axis=0, tiled=False)
-    q_run = lax.dynamic_index_in_dim(runs, z_at, 1, keepdims=False).reshape(T * Y)
-    k_run = lax.dynamic_index_in_dim(runs, y_at, 2, keepdims=False).reshape(T * Z)
+        jnp.broadcast_to(q_own, (YH,) + q_own.shape[1:]),
+        "yh",
+        split_axis=0,
+        concat_axis=0,
+        tiled=True,
+    )
+    near = lax.all_gather(kv_own, "z", axis=0, tiled=False)
+    far = lax.ppermute(near, "team", [(0, 1), (1, 0)])
+    kv_shape = (Z, X, YL, 2, PIECE, HD)
     partial = pl.pallas_call(
         attend_kernel,
-        out_shape=jax.ShapeDtypeStruct((T, Y, MSG, LANES), bf),
-        in_specs=[smem, smem, vmem, vmem],
+        out_shape=jax.ShapeDtypeStruct((YH, YL, MSG, LANES), bf),
+        in_specs=[smem, vmem, vmem, vmem],
         out_specs=vmem,
         scratch_shapes=[
             pltpu.VMEM((2 * KEYS, HD), bf),
@@ -241,31 +249,32 @@
         compiler_params=pltpu.CompilerParams(vmem_limit_bytes=24 << 20),
         name="attend",
     )(
-        q_run,
-        k_run,
-        q_all.reshape(Y, X, T, Q_ROWS, HD),
-        kv_all.reshape(Z, X, T, 2, PIECE, HD),
+        run_index,
+        q_all.reshape(YH, X, YL, Q_ROWS, HD),
+        near.reshape(kv_shape),
+        far.reshape(kv_shape),
     )
     parts = lax.all_to_all(
-        partial.reshape(T * Y, MSG, LANES), ("team", "y"), split_axis=0, concat_axis=0, tiled=True
+        partial.reshape(Y, MSG, LANES), ("yh", "yl"), split_axis=0, concat_axis=0, tiled=True
     )
     return pl.pallas_call(
         combine_kernel,
-        out_shape=jax.ShapeDtypeStruct((2 * HALF, T * GROUP, HD), bf),
+        out_shape=jax.ShapeDtypeStruct((2 * HALF, YL * GROUP, HD), bf),
         in_specs=[vmem],
         out_specs=vmem,
         compiler_params=pltpu.CompilerParams(vmem_limit_bytes=8 << 20),
         name="combine",
-    )(parts.reshape(T, Y, MSG, LANES))
+    )(parts.reshape(YH, YL, MSG, LANES))
 
 
 def solution(mesh):
-    split = Mesh(mesh.devices.reshape(X, T, Z, Y), ("heads", "team", "z", "y"))
-    spec = P("heads", ("team", "z", "y"), None, None)
+    axes = ("heads", "team", "z", "yh", "yl")
+    split = Mesh(mesh.devices.reshape(X, T, Z, YH, YL), axes)
+    spec = P("heads", axes[1:], None, None)
     return jax.shard_map(
         per_device,
         mesh=split,
         in_specs=(spec, spec, spec, P()),
-        out_specs=P(("team", "z", "y"), "heads", None),
+        out_specs=P(axes[1:], "heads", None),
         check_vma=False,
     )

time: 110 us -> 99.6 us (0.905)
  blocking collectives: 89.8 us -> 68.1 us
  starting transfers between devices: 3.69 us -> 14.5 us
  waiting for transfers between devices: 0.01 us -> 1.88 us
    all_to_all x2, blocking collectives: 60.7 us -> 35.7 us  [the longest x1 24.2 us: per_device(): lax.all_to_all(partial.reshape(Y, MSG, LANES), ('yh', 'yl'), split_axis=0...]
    ppermute x0 -> x1, starting transfers between devices: none -> 8.44 us  [per_device(): far = lax.ppermute(near, 'team', [(0, 1), (1, 0)])]
    all_gather x1, blocking collectives: 29.1 us -> 32.4 us  [per_device(): near = lax.all_gather(kv_own, 'z', axis=0, tiled=False)]
    all_to_all x1, starting transfers between devices: 3.69 us -> 6.02 us  [per_device(): lax.all_to_all(jnp.broadcast_to(q_own, (YH,) + q_own.shape[1:]), 'yh', sp...]
    ppermute x0 -> x1, waiting for transfers between devices: none -> 1.88 us  [per_device(): far = lax.ppermute(near, 'team', [(0, 1), (1, 0)])]
    unnamed x10 -> x8, local copies, waits for them, and re-layouts: 3.1 us -> 3.02 us
  transfers between devices with their start and end apart: 1 -> 2, of which waited for: 0 -> 1; matrix products, arithmetic and copies ran while one was open for 0% -> 0% of each run, Pallas kernels for 0% -> 0%
where the time goes in v3:
time: 99.6 us; the launch traced here: 99.2 us
  blocking collectives  68.1 us (68%)
  starting transfers between devices  14.5 us (15%)
  Pallas kernels  10.7 us (11%)
  local copies, waits for them, and re-layouts  3.89 us (4%)
  waiting for transfers between devices  1.88 us (2%)
    all_gather x1, blocking collectives, per_device(): near = lax.all_gather(kv_own, 'z', axis=0, tiled=False)  32.4 us
    all_to_all x1, blocking collectives, per_device(): lax.all_to_all(partial.reshape(Y, MSG, LANES), ('yh', 'yl'), split_axis=0...  24.2 us
    all_to_all x1, blocking collectives, per_device(): lax.all_to_all(packed, ('heads', 'yl'), split_axis=0, concat_axis=0, tile...  11.5 us
    pallas_call x1, Pallas kernels, per_device(): pl.pallas_call(attend_kernel, out_shape=jax.ShapeDtypeStruct((YH, YL, MSG...  9.12 us
    ppermute x1, starting transfers between devices, per_device(): far = lax.ppermute(near, 'team', [(0, 1), (1, 0)])  8.44 us
    all_to_all x1, starting transfers between devices, per_device(): lax.all_to_all(jnp.broadcast_to(q_own, (YH,) + q_own.shape[1:]), 'yh', sp...  6.02 us
    unnamed x8, local copies, waits for them, and re-layouts  3.02 us
  transfers between devices with their start and end apart: 2, of which 1 were waited for; matrix products, arithmetic and copies ran while one was open for 0% of the time, Pallas kernels for 0%

profile of v3, /device:TPU:1, one launch (start us, length us, event | category | flops | bytes accessed | tf_op | source)
XLA Modules:
  0.0 99.2 jit_solution(11851699651436819741)
XLA Ops:
  0.0 0.0 copy-start.3
  0.0 0.1 maximum_bitcast_fusion.freq_ref
  0.1 0.6 copy-done.3
  0.7 0.0 copy-start
  0.7 0.9 copy-done
  1.6 0.0 copy-start.1
  1.6 0.8 copy-done.1
  2.4 0.0 copy-start.2
  2.4 0.8 copy-done.2
  3.1 0.8 pack.1
  3.9 11.5 %all_to_all.15 = bf16[8,96,128]{2,1,0:T(8,128)(2,1)S(1)} all-to-all(bf16[8,96,128]{2,1,0:T(8,128)(2,1)S(1)} %pack.1), channel_id=1, replica_groups=mesh['heads'=4,'team'=2,'z'=12,'yh'=4,'yl'=2] {'heads','yl'}, dimensions={0} | all-to-all | bytes 393216 | tf_op jit(solution)/shard_map/all_to_all | solution.py:223
  15.4 0.9 broadcast_in_dim.12
  16.2 6.0 %all-to-all-start.1 = ((bf16[4,512,128]{2,1,0:T(8,128)(2,1)}), bf16[4,512,128]{2,1,0:T(8,128)(2,1)S(1)}, u32[]{:S(2)}, u32[]{:S(2)}) async-start(bf16[4,512,128]{2,1,0:T(8,128)(2,1)} %broadcast_in_dim.12), calls=%async_computation.1 | async-start | bytes 1048576 | tf_op jit(solution)/shard_map/all_to_all | solution.py:226
  22.3 32.4 %all_gather.3 = bf16[12,256,128]{2,1,0:T(8,128)(2,1)S(1)} all-gather(bf16[1,256,128]{2,1,0:T(8,128)(2,1)S(1)} %bitcast.15), channel_id=1, replica_groups=mesh['heads'=4,'team'=2,'z'=12,'yh'=4,'yl'=2] {'z'}, dimensions={0}, use_global_device_ids=true | all-gather | bytes 851968 | tf_op jit(solution)/shard_map/all_gather | solution.py:233
  54.7 8.4 %collective-permute-start = (bf16[12,256,128]{2,1,0:T(8,128)(2,1)S(1)}, bf16[12,256,128]{2,1,0:T(8,128)(2,1)S(1)}, u32[]{:S(2)}, u32[]{:S(2)}) collective-permute-start(bf16[12,256,128]{2,1,0:T(8,128)(2,1)S(1)} %all_gather.3), channel_id=1, source_target_pairs={{0,96},{96,0},{1,97},{97,1},{2,98},{98,2},{3,99},{99,3},{4,100},{1... | collective-permute-start | bytes 2359304 | tf_op jit(solution)/shard_map/ppermute | solution.py:234
  63.1 0.0 all-to-all-done.1
  63.1 1.9 %collective-permute-done = bf16[12,256,128]{2,1,0:T(8,128)(2,1)S(1)} collective-permute-done((bf16[12,256,128]{2,1,0:T(8,128)(2,1)S(1)}, bf16[12,256,128]{2,1,0:T(8,128)(2,1)S(1)}, u32[]{:S(2)}, u32[]{:S(2)}) %collective-permute-start) | collective-permute-done | bytes 786464 | tf_op jit(solution)/shard_map/ppermute | solution.py:234
  65.0 9.1 %attend.1 = bf16[4,2,272,128]{3,2,1,0:T(8,128)(2,1)S(1)} custom-call(s32[192]{0:T(256)S(1)} %copy-done.3, bf16[4,4,2,64,128]{4,3,2,1,0:T(8,128)(2,1)S(1)} %bitcast.12, bf16[12,4,2,2,16,128]{5,4,3,2,1,0:T(8,128)(2,1)S(1)} %bitcast.9, bf16[12,4,2,2,16,128]{5,4,3,2,1,0:T(8,128)(2,1)S(1)} %bitcast.13), custom_call_target="tpu_custom_call" | custom-call | tf_op jit(solution)/shard_map/attend/pallas_call | solution.py:236
  74.1 24.2 %all_to_all.16 = bf16[8,272,128]{2,1,0:T(8,128)(2,1)S(1)} all-to-all(bf16[8,272,128]{2,1,0:T(8,128)(2,1)S(1)} %bitcast.10), channel_id=1, replica_groups=mesh['heads'=4,'team'=2,'z'=12,'yh'=4,'yl'=2] {'yh','yl'}, dimensions={0} | all-to-all | bytes 1114112 | tf_op jit(solution)/shard_map/all_to_all | solution.py:257
  98.3 0.9 combine.1
  (3 shorter events, 0.0 us)
Async XLA Ops:
  0.0 0.7 copy-start.3
  0.7 0.9 copy-start
  1.6 0.8 copy-start.1
  2.4 0.8 copy-start.2
  16.2 46.9 %all-to-all-start.1 = ((bf16[4,512,128]{2,1,0:T(8,128)(2,1)}), bf16[4,512,128]{2,1,0:T(8,128)(2,1)S(1)}, u32[]{:S(2)}, u32[]{:S(2)}) async-start(bf16[4,512,128]{2,1,0:T(8,128)(2,1)} %broadcast_in_dim.12), calls=%async_computation.1 | async-start | bytes 1048576 | tf_op jit(solution)/shard_map/all_to_all | solution.py:226
  54.7 10.3 %collective-permute-start = (bf16[12,256,128]{2,1,0:T(8,128)(2,1)S(1)}, bf16[12,256,128]{2,1,0:T(8,128)(2,1)S(1)}, u32[]{:S(2)}, u32[]{:S(2)}) collective-permute-start(bf16[12,256,128]{2,1,0:T(8,128)(2,1)S(1)} %all_gather.3), channel_id=1, source_target_pairs={{0,96},{96,0},{1,97},{97,1},{2,98},{98,2},{3,99},{99,3},{4,100},{1... | collective-permute-start | bytes 2359304 | tf_op jit(solution)/shard_map/ppermute | solution.py:234

commit v4 on v3

--- a/solution.py
+++ b/solution.py
@@ -25,8 +25,9 @@
 PART = Z * YL * 2 * PIECE
 KEYS = T * PART
 LANES = 2 * Q_ROWS
+OWN = T * Z * YL
 MSG = 2 * HD + 16
-CHUNK = 128
+CHUNK = 1536
 PRODUCE_FIRST = 1
 LOG2_SCALE = HD ** -0.5 * math.log2(math.e)
 
@@ -42,8 +43,14 @@
     return jnp.where(wavelength < initial_context / high_factor, base_freq, middle)
 
 
-def pack_kernel(run_ref, freq_ref, q_ref, k_ref, v_ref, o_ref):
+def pack_kernel(run_ref, freq_ref, q_hbm, k_hbm, v_hbm, o_ref, q_ref, k_ref, v_ref, sems):
     f32 = jnp.float32
+    moves = [
+        pltpu.make_async_copy(src.at[0], dst, sems.at[i])
+        for i, (src, dst) in enumerate(((q_hbm, q_ref), (k_hbm, k_ref), (v_hbm, v_ref)))
+    ]
+    for move in moves:
+        move.start()
     x_at, t_at = lax.axis_index("heads"), lax.axis_index("team")
     z_at, y_at = lax.axis_index("z"), lax.axis_index("yh") * YL + lax.axis_index("yl")
     run = run_ref[(t_at * Z + z_at) * Y + y_at]
@@ -55,39 +62,62 @@
     sine = (jnp.sin(angles) * flip)[:, None, :]
 
     def turned(ref):
-        x = ref[0].astype(f32)
+        x = ref[...].astype(f32)
         y = x * cosine + jnp.roll(x, HD // 2, axis=-1) * sine
         return jnp.swapaxes(y, 0, 1).astype(jnp.bfloat16)
 
-    n_g = k_ref.shape[2]
-    q = turned(q_ref).reshape(n_g, GROUP * PIECE, HD)
-    o_ref[:, :Q_ROWS, :] = q
+    for move in moves:
+        move.wait()
+    n_g = k_ref.shape[1]
+    o_ref[:, :Q_ROWS, :] = turned(q_ref).reshape(n_g, GROUP * PIECE, HD)
     o_ref[:, Q_ROWS : Q_ROWS + PIECE, :] = turned(k_ref)
-    v = jnp.swapaxes(v_ref[0].astype(f32), 0, 1).astype(jnp.bfloat16)
+    v = jnp.swapaxes(v_ref[...].astype(f32), 0, 1).astype(jnp.bfloat16)
     o_ref[:, Q_ROWS + PIECE :, :] = v
 
 
-def attend_kernel(run_ref, q_ref, near_ref, far_ref, o_ref, k_s, vt_s, kpos_s, se_s, sl_s, w_s):
+def spread_kernel(mine_ref, q_ref, kv_ref):
+    q = mine_ref[:, :Q_ROWS, :].reshape(X * YL * Q_ROWS, HD)
+    for i in range(YH):
+        q_ref[i] = q
+    kv_ref[...] = mine_ref[:, Q_ROWS:, :].reshape(X * YL * 2 * PIECE, HD)
+
+
+def attend_kernel(run_ref, q_ref, near_ref, far_ref, o_ref, k_s, vt_s, own_s, se_s, sl_s, w_s):
     bf, f32 = jnp.bfloat16, jnp.float32
     t_at, z_at, yh_at = lax.axis_index("team"), lax.axis_index("z"), lax.axis_index("yh")
     row = lax.broadcasted_iota(jnp.int32, (PIECE, HD), 0)
+    col = lax.broadcasted_iota(jnp.int32, (PIECE, HD), 1)
+    lane = lax.broadcasted_iota(jnp.int32, (1, HD), 1)
+    k_runs = jnp.zeros((1, HD), jnp.int32)
     for part, kv_ref in enumerate((near_ref, far_ref)):
         team = t_at if part == 0 else 1 - t_at
         for half in range(2):
             picked = kv_ref[:, 2 * half : 2 * half + 2]
             start = half * KEYS + part * PART
             rows = slice(start, start + PART)
-            k_s[rows, :] = picked[:, :, :, 0].reshape(PART, HD)
+            k_s[rows, :HD] = picked[:, :, :, 0].reshape(PART, HD)
             vt_s[:, rows] = picked[:, :, :, 1].reshape(PART, HD).T
-            for z in range(Z):
-                for yl in range(YL):
-                    run = run_ref[((team * Z + z) * YH + yh_at) * YL + yl]
-                    base = (2 * SLOTS - 1 - run) * HALF if half else run * HALF
-                    for x in range(2):
-                        at = start + ((z * 2 + x) * YL + yl) * PIECE
-                        kpos_s[at : at + PIECE, :] = row + (base + x * PIECE)
-    lane = lax.broadcasted_iota(jnp.int32, (1, LANES), 1)
-    local = (lane // Q_ROWS) * PIECE + lane % PIECE
+        for z in range(Z):
+            for yl in range(YL):
+                slot = (part * Z + z) * YL + yl
+                run = run_ref[((team * Z + z) * YH + yh_at) * YL + yl]
+                k_runs = jnp.where(lane == slot, run, k_runs)
+                for x in range(2):
+                    hot = col == slot
+                    if part == 0:
+                        first = jnp.where(z_at == z, OWN + yl * HALF + x * PIECE, HD)
+                        hot = hot | (col == row + first)
+                    hot = jnp.where(hot, 1.0, 0.0).astype(bf)
+                    for half in range(2):
+                        at = half * KEYS + part * PART + ((z * 2 + x) * YL + yl) * PIECE
+                        k_s[at : at + PIECE, HD:] = hot
+    q_row = lax.broadcasted_iota(jnp.int32, (LANES, HD), 0)
+    q_local = (q_row // Q_ROWS) * PIECE + q_row % PIECE
+    k_local = lax.broadcasted_iota(jnp.int32, (LANES, HD), 1) - OWN
+    for yl in range(YL):
+        after = k_local - yl * HALF
+        hidden = (after > q_local) & (after < HALF)
+        own_s[yl] = jnp.where(hidden, mask_floor, 0.0)
 
     counts = (KEYS, 2 * KEYS)
     free = (0, KEYS)
@@ -97,21 +127,23 @@
             [q_ref[y, 2 * kind + x, t] for t in range(YL) for x in range(2)], axis=0
         )
 
-    def q_pos(kind, y):
-        runs = [run_ref[((t_at * Z + z_at) * YH + y) * YL + t] for t in range(YL)]
-        bases = [(2 * SLOTS - 1 - r) * HALF if kind else r * HALF for r in runs]
-        return jnp.concatenate([local + b for b in bases], axis=1)
+    def bias(kind, y):
+        own = jnp.where(y == yh_at, 1.0, 0.0)
+        blocks = []
+        for yl in range(YL):
+            run = run_ref[((t_at * Z + z_at) * YH + y) * YL + yl]
+            later = (k_runs < run) if kind else (k_runs > run)
+            hidden = jnp.where(later & (lane < OWN), mask_floor, 0.0)
+            blocks.append((own_s[yl] * own + hidden).astype(bf))
+        return jnp.concatenate(blocks, axis=0)
 
     def produce(kind, y, s_ref):
-        q_tile, pos, top = tile(kind, y), q_pos(kind, y), None
+        q_tile, top = tile(kind, y), None
+        q_wide = jnp.concatenate([q_tile, bias(kind, y)], axis=1)
         for at in range(0, counts[kind], CHUNK):
             rows = slice(at, at + CHUNK)
-            s = lax.dot_general(
-                k_s[rows, :], q_tile, (((1,), (1,)), ((), ())), preferred_element_type=f32
-            )
-            if at >= free[kind]:
-                kp = kpos_s[rows, :]
-                s = jnp.where(jnp.concatenate([kp, kp], axis=1) <= pos, s, mask_floor)
+            k, q = (k_s[rows, :], q_wide) if at >= free[kind] else (k_s[rows, :HD], q_tile)
+            s = lax.dot_general(k, q, (((1,), (1,)), ((), ())), preferred_element_type=f32)
             s_ref[rows, :] = s
             best = jnp.max(s.reshape(CHUNK // 8, 8, 2 * LANES), axis=0)
             top = best if top is None else jnp.maximum(top, best)
@@ -211,25 +243,31 @@
     bf, f32 = jnp.bfloat16, jnp.float32
     smem = pl.BlockSpec(memory_space=pltpu.SMEM)
     vmem = pl.BlockSpec(memory_space=pltpu.VMEM)
+    hbm = pl.BlockSpec(memory_space=pltpu.HBM)
     freqs = inverse_freqs(HD)
     packed = pl.pallas_call(
         pack_kernel,
         out_shape=jax.ShapeDtypeStruct((X * YL, (GROUP + 2) * PIECE, HD), bf),
-        in_specs=[smem, vmem, vmem, vmem, vmem],
+        in_specs=[smem, vmem, hbm, hbm, hbm],
         out_specs=vmem,
-        compiler_params=pltpu.CompilerParams(vmem_limit_bytes=8 << 20),
+        scratch_shapes=[pltpu.VMEM(a.shape[1:], bf) for a in (queries, keys, values)]
+        + [pltpu.SemaphoreType.DMA((3,))],
+        compiler_params=pltpu.CompilerParams(vmem_limit_bytes=60 << 20),
         name="pack",
     )(run_index, jnp.concatenate([freqs, freqs])[None, :], queries, keys, values)
     mine = lax.all_to_all(packed, ("heads", "yl"), split_axis=0, concat_axis=0, tiled=True)
-    q_own = mine[:, :Q_ROWS].reshape(1, X * YL * Q_ROWS, HD)
-    kv_own = mine[:, Q_ROWS:].reshape(X * YL * 2 * PIECE, HD)
-    q_all = lax.all_to_all(
-        jnp.broadcast_to(q_own, (YH,) + q_own.shape[1:]),
-        "yh",
-        split_axis=0,
-        concat_axis=0,
-        tiled=True,
-    )
+    q_own, kv_own = pl.pallas_call(
+        spread_kernel,
+        out_shape=(
+            jax.ShapeDtypeStruct((YH, X * YL * Q_ROWS, HD), bf),
+            jax.ShapeDtypeStruct((X * YL * 2 * PIECE, HD), bf),
+        ),
+        in_specs=[vmem],
+        out_specs=(vmem, vmem),
+        compiler_params=pltpu.CompilerParams(vmem_limit_bytes=8 << 20),
+        name="spread",
+    )(mine)
+    q_all = lax.all_to_all(q_own, "yh", split_axis=0, concat_axis=0, tiled=True)
     near = lax.all_gather(kv_own, "z", axis=0, tiled=False)
     far = lax.ppermute(near, "team", [(0, 1), (1, 0)])
     kv_shape = (Z, X, YL, 2, PIECE, HD)
@@ -239,9 +277,9 @@
         in_specs=[smem, vmem, vmem, vmem],
         out_specs=vmem,
         scratch_shapes=[
-            pltpu.VMEM((2 * KEYS, HD), bf),
+            pltpu.VMEM((2 * KEYS, 2 * HD), bf),
             pltpu.VMEM((HD, 2 * KEYS), bf),
-            pltpu.VMEM((2 * KEYS, HD), jnp.int32),
+            pltpu.VMEM((YL, LANES, HD), f32),
             pltpu.VMEM((KEYS, 2 * LANES), f32),
             pltpu.VMEM((2 * KEYS, 2 * LANES), f32),
             pltpu.VMEM((2, 2 * KEYS, 2 * LANES), bf),

time: 99.6 us -> 98.8 us (level)
  local copies, waits for them, and re-layouts: 3.89 us -> 0.68 us
  Pallas kernels: 10.7 us -> 12.5 us
    unnamed x8 -> x2, local copies, waits for them, and re-layouts: 3.02 us -> 0.68 us
    pallas_call x1, Pallas kernels: 0.77 us -> 2.47 us  [per_device(): pl.pallas_call(pack_kernel, out_shape=jax.ShapeDtypeStruct((X * YL, (GROU...]
where the time goes in v4:
time: 98.8 us; the launch traced here: 98.4 us
  blocking collectives  68.5 us (69%)
  starting transfers between devices  14.3 us (14%)
  Pallas kernels  12.5 us (13%)
  waiting for transfers between devices  1.88 us (2%)
    all_gather x1, blocking collectives, per_device(): near = lax.all_gather(kv_own, 'z', axis=0, tiled=False)  32.4 us
    all_to_all x1, blocking collectives, per_device(): lax.all_to_all(partial.reshape(Y, MSG, LANES), ('yh', 'yl'), split_axis=0...  24.4 us
    all_to_all x1, blocking collectives, per_device(): lax.all_to_all(packed, ('heads', 'yl'), split_axis=0, concat_axis=0, tile...  11.7 us
    ppermute x1, starting transfers between devices, per_device(): far = lax.ppermute(near, 'team', [(0, 1), (1, 0)])  8.26 us
    pallas_call x1, Pallas kernels, per_device(): pl.pallas_call(attend_kernel, out_shape=jax.ShapeDtypeStruct((YH, YL, MSG...  8.25 us
    all_to_all x1, starting transfers between devices, per_device(): q_all = lax.all_to_all(q_own, 'yh', split_axis=0, concat_axis=0, tiled=True)  6.02 us
    pallas_call x1, Pallas kernels, per_device(): pl.pallas_call(pack_kernel, out_shape=jax.ShapeDtypeStruct((X * YL, (GROU...  2.47 us
  transfers between devices with their start and end apart: 2, of which 1 were waited for; matrix products, arithmetic and copies ran while one was open for 0% of the time, Pallas kernels for 0%

profile of v4, /device:TPU:1, one launch (start us, length us, event | category | flops | bytes accessed | tf_op | source)
XLA Modules:
  0.0 98.4 jit_solution(4017745063612632933)
XLA Ops:
  0.0 0.6 maximum_bitcast_fusion.freq_ref
  0.6 2.5 %pack.1 = bf16[8,96,128]{2,1,0:T(8,128)(2,1)} custom-call(s32[192]{0:T(256)} %run_ref.3, f32[1,128]{1,0:T(1,128)} %maximum_bitcast_fusion.freq_ref, bf16[1,16,32,128]{3,2,1,0:T(8,128)(2,1)} %q_hbm.1, bf16[1,16,8,128]{3,2,1,0:T(8,128)(2,1)} %k_hbm.1, bf16[1,16,8,128]{3,2,1,0:T(8,128)(2,1)} %v_hbm.1), custom_call_target="tpu_custom_call" | custom-call | tf_op jit(solution)/shard_map/pack/pallas_call | solution.py:248
  3.1 11.7 %all_to_all.15.mine_ref = bf16[8,96,128]{2,1,0:T(8,128)(2,1)S(1)} all-to-all(bf16[8,96,128]{2,1,0:T(8,128)(2,1)} %pack.1), channel_id=1, replica_groups=mesh['heads'=4,'team'=2,'z'=12,'yh'=4,'yl'=2] {'heads','yl'}, dimensions={0} | all-to-all | bytes 393216 | tf_op jit(solution)/shard_map/all_to_all | solution.py:258
  14.8 0.9 spread.1
  15.6 6.0 %all-to-all-start.1 = ((bf16[4,512,128]{2,1,0:T(8,128)(2,1)}), bf16[4,512,128]{2,1,0:T(8,128)(2,1)S(1)}, u32[]{:S(2)}, u32[]{:S(2)}) async-start(bf16[4,512,128]{2,1,0:T(8,128)(2,1)} %get-tuple-element.7), calls=%async_computation.1 | async-start | bytes 1048576 | tf_op jit(solution)/shard_map/all_to_all | solution.py:270
  21.7 32.4 %all-gather = bf16[3072,128]{1,0:T(8,128)(2,1)S(1)} all-gather(bf16[256,128]{1,0:T(8,128)(2,1)S(1)} %get-tuple-element.8), channel_id=2, replica_groups=mesh['heads'=4,'team'=2,'z'=12,'yh'=4,'yl'=2] {'z'}, dimensions={0}, use_global_device_ids=true | all-gather | bytes 851968 | tf_op jit(solution)/shard_map/all_gather | solution.py:271
  54.0 8.3 %collective-permute-start = (bf16[12,256,128]{2,1,0:T(8,128)(2,1)S(1)}, bf16[12,256,128]{2,1,0:T(8,128)(2,1)S(1)}, u32[]{:S(2)}, u32[]{:S(2)}) collective-permute-start(bf16[12,256,128]{2,1,0:T(8,128)(2,1)S(1)} %bitcast.8), channel_id=1, source_target_pairs={{0,96},{96,0},{1,97},{97,1},{2,98},{98,2},{3,99},{99,3},{4,100},{1... | collective-permute-start | bytes 2359304 | tf_op jit(solution)/shard_map/ppermute | solution.py:272
  62.3 0.0 all-to-all-done.1
  62.3 1.9 %collective-permute-done = bf16[12,256,128]{2,1,0:T(8,128)(2,1)S(1)} collective-permute-done((bf16[12,256,128]{2,1,0:T(8,128)(2,1)S(1)}, bf16[12,256,128]{2,1,0:T(8,128)(2,1)S(1)}, u32[]{:S(2)}, u32[]{:S(2)}) %collective-permute-start) | collective-permute-done | bytes 786464 | tf_op jit(solution)/shard_map/ppermute | solution.py:272
  64.2 0.0 copy-start
  64.2 0.7 copy-done
  64.9 8.2 %attend.1 = bf16[4,2,272,128]{3,2,1,0:T(8,128)(2,1)S(1)} custom-call(s32[192]{0:T(256)S(1)} %copy-done, bf16[4,4,2,64,128]{4,3,2,1,0:T(8,128)(2,1)S(1)} %bitcast.12, bf16[12,4,2,2,16,128]{5,4,3,2,1,0:T(8,128)(2,1)S(1)} %bitcast.9, bf16[12,4,2,2,16,128]{5,4,3,2,1,0:T(8,128)(2,1)S(1)} %bitcast.13), custom_call_target="tpu_custom_call" | custom-call | tf_op jit(solution)/shard_map/attend/pallas_call | solution.py:274
  73.1 24.4 %all_to_all.16 = bf16[8,272,128]{2,1,0:T(8,128)(2,1)S(1)} all-to-all(bf16[8,272,128]{2,1,0:T(8,128)(2,1)S(1)} %bitcast.10), channel_id=1, replica_groups=mesh['heads'=4,'team'=2,'z'=12,'yh'=4,'yl'=2] {'yh','yl'}, dimensions={0} | all-to-all | bytes 1114112 | tf_op jit(solution)/shard_map/all_to_all | solution.py:295
  97.6 0.9 combine.1
  (1 shorter events, 0.0 us)
Async XLA Ops:
  15.6 46.7 %all-to-all-start.1 = ((bf16[4,512,128]{2,1,0:T(8,128)(2,1)}), bf16[4,512,128]{2,1,0:T(8,128)(2,1)S(1)}, u32[]{:S(2)}, u32[]{:S(2)}) async-start(bf16[4,512,128]{2,1,0:T(8,128)(2,1)} %get-tuple-element.7), calls=%async_computation.1 | async-start | bytes 1048576 | tf_op jit(solution)/shard_map/all_to_all | solution.py:270
  54.0 10.2 %collective-permute-start = (bf16[12,256,128]{2,1,0:T(8,128)(2,1)S(1)}, bf16[12,256,128]{2,1,0:T(8,128)(2,1)S(1)}, u32[]{:S(2)}, u32[]{:S(2)}) collective-permute-start(bf16[12,256,128]{2,1,0:T(8,128)(2,1)S(1)} %bitcast.8), channel_id=1, source_target_pairs={{0,96},{96,0},{1,97},{97,1},{2,98},{98,2},{3,99},{99,3},{4,100},{1... | collective-permute-start | bytes 2359304 | tf_op jit(solution)/shard_map/ppermute | solution.py:272
  64.2 0.7 copy-start

commit v5 on v4

v5 whole, which is shorter than its diff:
```python
import functools
import math

import jax
import jax.numpy as jnp
import numpy as np
from jax import lax
from jax.experimental import pallas as pl
from jax.experimental.pallas import tpu as pltpu
from jax.sharding import Mesh, PartitionSpec as P

mask_floor = -1e30
rope_theta = 500000.0
rope_factor = 8.0
low_factor = 1.0
high_factor = 4.0
initial_context = 8192.0

X, T, Z, YH, YL = 4, 2, 12, 4, 2
Y = YH * YL
PIECE = 16
HALF = 32
GROUP = 4
HD = 128
SLOTS = T * Z * Y
Q_ROWS = GROUP * PIECE
PART = Z * YL * 2 * PIECE
LANES = 2 * Q_ROWS
OWN = Z * YL
MSG = 2 * HD + 8
LOG2_SCALE = HD ** -0.5 * math.log2(math.e)


def inverse_freqs():
    counter = np.arange(HD // 2, dtype=np.float64)
    base_freq = 1.0 / rope_theta ** (2.0 * counter / HD)
    wavelength = 2.0 * np.pi / base_freq
    smooth = (initial_context / wavelength - low_factor) / (high_factor - low_factor)
    blended = (1.0 - smooth) * base_freq / rope_factor + smooth * base_freq
    middle = np.where(wavelength > initial_context / low_factor, base_freq / rope_factor, blended)
    freqs = np.where(wavelength < initial_context / high_factor, base_freq, middle)
    return np.concatenate([freqs, freqs])[None, :].astype(np.float32)


def pack_kernel(run_ref, freq_ref, q_hbm, k_hbm, v_hbm, o_ref, q_ref, k_ref, v_ref, sems):
    f32 = jnp.float32
    moves = [
        pltpu.make_async_copy(src.at[0], dst, sems.at[i])
        for i, (src, dst) in enumerate(((q_hbm, q_ref), (k_hbm, k_ref), (v_hbm, v_ref)))
    ]
    for move in moves:
        move.start()
    x_at, t_at = lax.axis_index("heads"), lax.axis_index("team")
    z_at, y_at = lax.axis_index("z"), lax.axis_index("yh") * YL + lax.axis_index("yl")
    run = run_ref[(t_at * Z + z_at) * Y + y_at]
    base = jnp.where(x_at < 2, run * HALF, (2 * SLOTS - 1 - run) * HALF - HALF) + x_at * PIECE
    pos = lax.broadcasted_iota(jnp.int32, (PIECE, HD), 0) + base
    angles = pos.astype(f32) * freq_ref[...]
    cosine = jnp.cos(angles)[:, None, :]
    flip = jnp.where(lax.broadcasted_iota(jnp.int32, (PIECE, HD), 1) < HD // 2, -1.0, 1.0)
    sine = (jnp.sin(angles) * flip)[:, None, :]

    def turned(ref):
        x = ref[...].astype(f32)
        y = x * cosine + jnp.roll(x, HD // 2, axis=-1) * sine
        return jnp.swapaxes(y, 0, 1).astype(jnp.bfloat16)

    for move in moves:
        move.wait()
    n_g = k_ref.shape[1]
    o_ref[:, :Q_ROWS, :] = turned(q_ref).reshape(n_g, GROUP * PIECE, HD)
    o_ref[:, Q_ROWS : Q_ROWS + PIECE, :] = turned(k_ref)
    v = jnp.swapaxes(v_ref[...].astype(f32), 0, 1).astype(jnp.bfloat16)
    o_ref[:, Q_ROWS + PIECE :, :] = v


def spread_kernel(mine_ref, q_ref, kv_ref):
    q = mine_ref[:, :Q_ROWS, :].reshape(X * YL * Q_ROWS, HD)
    for i in range(YH):
        q_ref[i] = q
    kv_ref[...] = mine_ref[:, Q_ROWS:, :].reshape(X * YL * 2 * PIECE, HD)


def attend_kernel(part, run_ref, q_ref, kv_ref, *refs):
    bf, f32 = jnp.bfloat16, jnp.float32
    if part == 0:
        acc_ref, st_ref, k_s, vt_s, se_s, sl_s, w_s, own_s = refs
    else:
        acc_ref, st_ref, o_ref, k_s, vt_s, se_s, sl_s, w_s = refs
    t_at, z_at, yh_at = lax.axis_index("team"), lax.axis_index("z"), lax.axis_index("yh")
    row = lax.broadcasted_iota(jnp.int32, (PIECE, HD), 0)
    col = lax.broadcasted_iota(jnp.int32, (PIECE, HD), 1)
    lane = lax.broadcasted_iota(jnp.int32, (1, HD), 1)
    k_runs = jnp.zeros((1, HD), jnp.int32)
    team = t_at if part == 0 else 1 - t_at
    for half in range(2):
        picked = kv_ref[:, 2 * half : 2 * half + 2]
        rows = slice(half * PART, (half + 1) * PART)
        k_s[rows, :HD] = picked[:, :, :, 0].reshape(PART, HD)
        vt_s[:, rows] = picked[:, :, :, 1].reshape(PART, HD).T
    for z in range(Z):
        for yl in range(YL):
            slot = z * YL + yl
            run = run_ref[((team * Z + z) * YH + yh_at) * YL + yl]
            k_runs = jnp.where(lane == slot, run, k_runs)
            for x in range(2):
                hot = col == slot
                if part == 0:
                    first = jnp.where(z_at == z, OWN + yl * HALF + x * PIECE, HD)
                    hot = hot | (col == row + first)
                hot = jnp.where(hot, 1.0, 0.0).astype(bf)
                for half in range(2):
                    at = half * PART + ((z * 2 + x) * YL + yl) * PIECE
                    k_s[at : at + PIECE, HD:] = hot
    if part == 0:
        q_row = lax.broadcasted_iota(jnp.int32, (LANES, HD), 0)
        q_local = (q_row // Q_ROWS) * PIECE + q_row % PIECE
        k_local = lax.broadcasted_iota(jnp.int32, (LANES, HD), 1) - OWN
        for yl in range(YL):
            after = k_local - yl * HALF
            hidden = (after > q_local) & (after < HALF)
            own_s[yl] = jnp.where(hidden, mask_floor, 0.0)

    def tile(kind, y):
        return jnp.concatenate(
            [q_ref[y, 2 * kind + x, t] for t in range(YL) for x in range(2)], axis=0
        )

    def bias(kind, y):
        blocks = []
        for yl in range(YL):
            run = run_ref[((t_at * Z + z_at) * YH + y) * YL + yl]
            later = (k_runs < run) if kind else (k_runs > run)
            hidden = jnp.where(later & (lane < OWN), mask_floor, 0.0)
            if part == 0:
                hidden = own_s[yl] * jnp.where(y == yh_at, 1.0, 0.0) + hidden
            blocks.append(jnp.broadcast_to(hidden, (LANES, HD)).astype(bf))
        return jnp.concatenate(blocks, axis=0)

    def produce(kind, y, s_ref):
        q_tile = tile(kind, y)
        q_wide = jnp.concatenate([q_tile, bias(kind, y)], axis=1)
        pieces = [(slice(kind * PART, (kind + 1) * PART), q_wide)]
        if kind:
            pieces.append((slice(0, PART), q_tile))
        top = None
        for rows, q in pieces:
            s = lax.dot_general(
                k_s[rows, : q.shape[1]], q, (((1,), (1,)), ((), ())), preferred_element_type=f32
            )
            s_ref[rows, :] = s
            best = jnp.max(s.reshape(PART // 8, 8, 2 * LANES), axis=0)
            top = best if top is None else jnp.maximum(top, best)
        return jnp.max(top, axis=0, keepdims=True)

    def consume(kind, y, s_ref, top):
        total = jnp.zeros((8, 2 * LANES), f32)
        n = (kind + 1) * PART
        for at in range(0, n, PART):
            rows = slice(at, at + PART)
            w = jnp.exp2((s_ref[rows, :] - top) * LOG2_SCALE)
            total = total + jnp.sum(w.reshape(PART // 8, 8, 2 * LANES), axis=0)
            w_s[kind, rows, :] = w.astype(bf)
        total = jnp.sum(total, axis=0, keepdims=True)
        o = lax.dot_general(
            vt_s[:, :n], w_s[kind, :n, :], (((1,), (0,)), ((), ())), preferred_element_type=f32
        )
        if part == 0:
            acc_ref[y, kind] = o
            st_ref[y, kind, 0:1, :] = top
            st_ref[y, kind, 1:2, :] = total
            return None
        before = st_ref[y, kind, 0:1, :]
        best = jnp.maximum(top, before)
        keep = jnp.exp2((before - best) * LOG2_SCALE)
        add = jnp.exp2((top - best) * LOG2_SCALE)
        total = total * add + st_ref[y, kind, 1:2, :] * keep
        scale = 1.0 / total
        o = (o * (add * scale) + acc_ref[y, kind] * (keep * scale)).astype(bf)
        for t in range(YL):
            cols = slice(t * LANES, (t + 1) * LANES)
            o_ref[y, t, kind * HD : (kind + 1) * HD, :] = o[:, cols]
        lse = best * LOG2_SCALE + jnp.log2(total)
        hi = lse.astype(bf).astype(f32)
        mid = (lse - hi).astype(bf).astype(f32)
        return [hi, mid, lse - hi - mid]

    def step(y, top_e):
        top_l = produce(1, y, sl_s)
        early = consume(0, y, se_s, top_e)
        top_e = produce(0, jnp.minimum(y + 1, YH - 1), se_s)
        late = consume(1, y, sl_s, top_l)
        if part == 1:
            pad = jnp.zeros((2, 2 * LANES), f32)
            stats = jnp.concatenate(early + late + [pad], axis=0).astype(bf)
            for t in range(YL):
                o_ref[y, t, 2 * HD :, :] = stats[:, t * LANES : (t + 1) * LANES]
        return top_e

    lax.fori_loop(0, YH, step, produce(0, 0, se_s))


def combine_kernel(r_ref, o_ref):
    f32 = jnp.float32
    for half in range(2):
        heads = []
        for t in range(YL):
            lse = []
            for y in range(YH):
                st = r_ref[y, t, 2 * HD :, :].astype(f32)
                at = 3 * half
                lse.append(st[at : at + 1] + st[at + 1 : at + 2] + st[at + 2 : at + 3])
            top = lse[0]
            for v in lse[1:]:
                top = jnp.maximum(top, v)
            ws = [jnp.exp2(v - top) for v in lse]
            total = ws[0]
            for v in ws[1:]:
                total = total + v
            acc = jnp.zeros((HD, LANES), f32)
            for y in range(YH):
                acc = acc + r_ref[y, t, half * HD : (half + 1) * HD, :].astype(f32) * ws[y]
            heads.append((acc * (1.0 / total)).T)
        for p in range(2):
            block = jnp.stack(
                [
                    heads[t][p * Q_ROWS + j * PIECE : p * Q_ROWS + (j + 1) * PIECE]
                    for t in range(YL)
                    for j in range(GROUP)
                ],
                axis=0,
            )
            at = half * HALF + p * PIECE
            o_ref[at : at + PIECE] = jnp.swapaxes(block, 0, 1).astype(jnp.bfloat16)


def per_device(queries, keys, values, run_index):
    bf, f32 = jnp.bfloat16, jnp.float32
    smem = pl.BlockSpec(memory_space=pltpu.SMEM)
    vmem = pl.BlockSpec(memory_space=pltpu.VMEM)
    hbm = pl.BlockSpec(memory_space=pltpu.HBM)
    packed = pl.pallas_call(
        pack_kernel,
        out_shape=jax.ShapeDtypeStruct((X * YL, (GROUP + 2) * PIECE, HD), bf),
        in_specs=[smem, vmem, hbm, hbm, hbm],
        out_specs=vmem,
        scratch_shapes=[pltpu.VMEM(a.shape[1:], bf) for a in (queries, keys, values)]
        + [pltpu.SemaphoreType.DMA((3,))],
        compiler_params=pltpu.CompilerParams(vmem_limit_bytes=60 << 20),
        name="pack",
    )(run_index, inverse_freqs(), queries, keys, values)
    mine = lax.all_to_all(packed, ("heads", "yl"), split_axis=0, concat_axis=0, tiled=True)
    q_own, kv_own = pl.pallas_call(
        spread_kernel,
        out_shape=(
            jax.ShapeDtypeStruct((YH, X * YL * Q_ROWS, HD), bf),
            jax.ShapeDtypeStruct((X * YL * 2 * PIECE, HD), bf),
        ),
        in_specs=[vmem],
        out_specs=(vmem, vmem),
        compiler_params=pltpu.CompilerParams(vmem_limit_bytes=8 << 20),
        name="spread",
    )(mine)
    q_all = lax.all_to_all(q_own, "yh", split_axis=0, concat_axis=0, tiled=True)
    near = lax.all_gather(kv_own, "z", axis=0, tiled=False)
    far = lax.ppermute(near, "team", [(0, 1), (1, 0)])
    kv_shape = (Z, X, YL, 2, PIECE, HD)
    q_all = q_all.reshape(YH, X, YL, Q_ROWS, HD)
    f32 = jnp.float32

    def attend(part, kv, *state):
        if part == 0:
            out = (
                jax.ShapeDtypeStruct((YH, 2, HD, 2 * LANES), f32),
                jax.ShapeDtypeStruct((YH, 2, 8, 2 * LANES), f32),
            )
        else:
            out = jax.ShapeDtypeStruct((YH, YL, MSG, LANES), bf)
        scratch = [
            pltpu.VMEM((2 * PART, 2 * HD), bf),
            pltpu.VMEM((HD, 2 * PART), bf),
            pltpu.VMEM((PART, 2 * LANES), f32),
            pltpu.VMEM((2 * PART, 2 * LANES), f32),
            pltpu.VMEM((2, 2 * PART, 2 * LANES), bf),
        ]
        return pl.pallas_call(
            functools.partial(attend_kernel, part),
            out_shape=out,
            in_specs=[smem, vmem, vmem] + [vmem] * len(state),
            out_specs=(vmem, vmem) if part == 0 else vmem,
            scratch_shapes=scratch + [pltpu.VMEM((YL, LANES, HD), f32)] * (part == 0),
            compiler_params=pltpu.CompilerParams(vmem_limit_bytes=20 << 20),
            name=("attend_near", "attend_far")[part],
        )(run_index, q_all, kv.reshape(kv_shape), *state)

    partial = attend(1, far, *attend(0, near))
    parts = lax.all_to_all(
        partial.reshape(Y, MSG, LANES), ("yh", "yl"), split_axis=0, concat_axis=0, tiled=True
    )
    return pl.pallas_call(
        combine_kernel,
        out_shape=jax.ShapeDtypeStruct((2 * HALF, YL * GROUP, HD), bf),
        in_specs=[vmem],
        out_specs=vmem,
        compiler_params=pltpu.CompilerParams(vmem_limit_bytes=8 << 20),
        name="combine",
    )(parts.reshape(YH, YL, MSG, LANES))


def solution(mesh):
    axes = ("heads", "team", "z", "yh", "yl")
    split = Mesh(mesh.devices.reshape(X, T, Z, YH, YL), axes)
    spec = P("heads", axes[1:], None, None)
    return jax.shard_map(
        per_device,
        mesh=split,
        in_specs=(spec, spec, spec, P()),
        out_specs=P(axes[1:], "heads", None),
        check_vma=False,
    )
```

time: 98.8 us -> 98.2 us (level)
  waiting for transfers between devices: 1.88 us -> 0.01 us
  Pallas kernels: 12.5 us -> 13.8 us
    ppermute x1, waiting for transfers between devices: 1.88 us -> 0.01 us  [per_device(): far = lax.ppermute(near, 'team', [(0, 1), (1, 0)])]
    pallas_call x1 -> x2, Pallas kernels: 8.25 us -> 9.6 us  [attend(): pl.pallas_call(functools.partial(attend_kernel, part), out_shape=out, in_...]
  transfers between devices with their start and end apart: 2 -> 2, of which waited for: 1 -> 0; matrix products, arithmetic and copies ran while one was open for 0% -> 0% of each run, Pallas kernels for 0% -> 5%
where the time goes in v5:
time: 98.2 us; the launch traced here: 97.8 us
  blocking collectives  69 us (70%)
  starting transfers between devices  14.3 us (15%)
  Pallas kernels  13.8 us (14%)
    all_gather x1, blocking collectives, per_device(): near = lax.all_gather(kv_own, 'z', axis=0, tiled=False)  32.4 us
    all_to_all x1, blocking collectives, per_device(): lax.all_to_all(partial.reshape(Y, MSG, LANES), ('yh', 'yl'), split_axis=0...  25 us
    all_to_all x1, blocking collectives, per_device(): lax.all_to_all(packed, ('heads', 'yl'), split_axis=0, concat_axis=0, tile...  11.7 us
    pallas_call x2, Pallas kernels, attend(): pl.pallas_call(functools.partial(attend_kernel, part), out_shape=out, in_...  9.6 us
    ppermute x1, starting transfers between devices, per_device(): far = lax.ppermute(near, 'team', [(0, 1), (1, 0)])  8.26 us
    all_to_all x1, starting transfers between devices, per_device(): q_all = lax.all_to_all(q_own, 'yh', split_axis=0, concat_axis=0, tiled=True)  6.02 us
    pallas_call x1, Pallas kernels, per_device(): pl.pallas_call(pack_kernel, out_shape=jax.ShapeDtypeStruct((X * YL, (GROU...  2.47 us
  transfers between devices with their start and end apart: 2, of which 0 were waited for; matrix products, arithmetic and copies ran while one was open for 0% of the time, Pallas kernels for 5%

profile of v5, /device:TPU:1, one launch (start us, length us, event | category | flops | bytes accessed | tf_op | source)
XLA Modules:
  0.0 97.8 jit_solution(4740878412496340117)
XLA Ops:
  0.0 2.5 %pack.1 = bf16[8,96,128]{2,1,0:T(8,128)(2,1)} custom-call(s32[192]{0:T(256)} %run_ref.5, f32[1,128]{1,0:T(1,128)} %constant.2.clone.freq_ref, bf16[1,16,32,128]{3,2,1,0:T(8,128)(2,1)} %q_hbm.1, bf16[1,16,8,128]{3,2,1,0:T(8,128)(2,1)} %k_hbm.1, bf16[1,16,8,128]{3,2,1,0:T(8,128)(2,1)} %v_hbm.1), custom_call_target="tpu_custom_call" | custom-call | tf_op jit(solution)/shard_map/pack/pallas_call | solution.py:242
  2.5 11.7 %all_to_all.15.mine_ref = bf16[8,96,128]{2,1,0:T(8,128)(2,1)S(1)} all-to-all(bf16[8,96,128]{2,1,0:T(8,128)(2,1)} %pack.1), channel_id=1, replica_groups=mesh['heads'=4,'team'=2,'z'=12,'yh'=4,'yl'=2] {'heads','yl'}, dimensions={0} | all-to-all | bytes 393216 | tf_op jit(solution)/shard_map/all_to_all | solution.py:252
  14.1 0.9 spread.1
  15.0 6.0 %all-to-all-start.1 = ((bf16[4,512,128]{2,1,0:T(8,128)(2,1)}), bf16[4,512,128]{2,1,0:T(8,128)(2,1)S(1)}, u32[]{:S(2)}, u32[]{:S(2)}) async-start(bf16[4,512,128]{2,1,0:T(8,128)(2,1)} %get-tuple-element.9), calls=%async_computation.1 | async-start | bytes 1048576 | tf_op jit(solution)/shard_map/all_to_all | solution.py:264
  21.0 32.4 %all-gather = bf16[3072,128]{1,0:T(8,128)(2,1)S(1)} all-gather(bf16[256,128]{1,0:T(8,128)(2,1)S(1)} %get-tuple-element.10), channel_id=2, replica_groups=mesh['heads'=4,'team'=2,'z'=12,'yh'=4,'yl'=2] {'z'}, dimensions={0}, use_global_device_ids=true | all-gather | bytes 851968 | tf_op jit(solution)/shard_map/all_gather | solution.py:265
  53.4 8.3 %collective-permute-start = (bf16[12,256,128]{2,1,0:T(8,128)(2,1)S(1)}, bf16[12,256,128]{2,1,0:T(8,128)(2,1)S(1)}, u32[]{:S(2)}, u32[]{:S(2)}) collective-permute-start(bf16[12,256,128]{2,1,0:T(8,128)(2,1)S(1)} %bitcast.8), channel_id=1, source_target_pairs={{0,96},{96,0},{1,97},{97,1},{2,98},{98,2},{3,99},{99,3},{4,100},{1... | collective-permute-start | bytes 2359304 | tf_op jit(solution)/shard_map/ppermute | solution.py:266
  61.7 0.0 all-to-all-done.1
  61.7 0.0 copy-start
  61.7 0.7 copy-done
  62.4 4.7 %attend_near.1 = (f32[4,2,128,256]{3,2,1,0:T(8,128)S(1)}, f32[4,2,8,256]{3,2,1,0:T(8,128)S(1)}) custom-call(s32[192]{0:T(256)S(1)} %copy-done, bf16[4,4,2,64,128]{4,3,2,1,0:T(8,128)(2,1)S(1)} %bitcast.6, bf16[12,4,2,2,16,128]{5,4,3,2,1,0:T(8,128)(2,1)S(1)} %bitcast.9), custom_call_target="tpu_custom_call" | custom-call | tf_op jit(solution)/shard_map/attend_near/pallas_call | solution.py:286
  67.1 0.0 collective-permute-done
  67.1 4.9 %attend_far.1 = bf16[4,2,264,128]{3,2,1,0:T(8,128)(2,1)S(1)} custom-call(s32[192]{0:T(256)S(1)} %copy-done, bf16[4,4,2,64,128]{4,3,2,1,0:T(8,128)(2,1)S(1)} %bitcast.7, bf16[12,4,2,2,16,128]{5,4,3,2,1,0:T(8,128)(2,1)S(1)} %bitcast.12, f32[4,2,128,256]{3,2,1,0:T(8,128)S(1)} %get-tuple-element.11.refs_0_, f32[4,2,8,256]{3,2,1,0:T(8,128)S(1)} %get-tuple-element.12.refs_1_), custom_call_target="tpu_custom_call" | custom-call | tf_op jit(solution)/shard_map/attend_far/pallas_call | solution.py:286
  72.0 25.0 %all_to_all.16 = bf16[8,264,128]{2,1,0:T(8,128)(2,1)S(1)} all-to-all(bf16[8,264,128]{2,1,0:T(8,128)(2,1)S(1)} %bitcast.10), channel_id=1, replica_groups=mesh['heads'=4,'team'=2,'z'=12,'yh'=4,'yl'=2] {'yh','yl'}, dimensions={0} | all-to-all | bytes 1081344 | tf_op jit(solution)/shard_map/all_to_all | solution.py:297
  97.0 0.9 combine.1
Async XLA Ops:
  15.0 46.7 %all-to-all-start.1 = ((bf16[4,512,128]{2,1,0:T(8,128)(2,1)}), bf16[4,512,128]{2,1,0:T(8,128)(2,1)S(1)}, u32[]{:S(2)}, u32[]{:S(2)}) async-start(bf16[4,512,128]{2,1,0:T(8,128)(2,1)} %get-tuple-element.9), calls=%async_computation.1 | async-start | bytes 1048576 | tf_op jit(solution)/shard_map/all_to_all | solution.py:264
  53.4 13.7 %collective-permute-start = (bf16[12,256,128]{2,1,0:T(8,128)(2,1)S(1)}, bf16[12,256,128]{2,1,0:T(8,128)(2,1)S(1)}, u32[]{:S(2)}, u32[]{:S(2)}) collective-permute-start(bf16[12,256,128]{2,1,0:T(8,128)(2,1)S(1)} %bitcast.8), channel_id=1, source_target_pairs={{0,96},{96,0},{1,97},{97,1},{2,98},{98,2},{3,99},{99,3},{4,100},{1... | collective-permute-start | bytes 2359304 | tf_op jit(solution)/shard_map/ppermute | solution.py:266
  61.7 0.7 copy-start

commit v6 on v5

--- a/solution.py
+++ b/solution.py
@@ -42,14 +42,22 @@
     return np.concatenate([freqs, freqs])[None, :].astype(np.float32)
 
 
-def pack_kernel(run_ref, freq_ref, q_hbm, k_hbm, v_hbm, o_ref, q_ref, k_ref, v_ref, sems):
+def pack_kernel(
+    run_hbm, freq_hbm, q_hbm, k_hbm, v_hbm, o_ref, run_ref, freq_ref, q_ref, k_ref, v_ref, sems
+):
     f32 = jnp.float32
-    moves = [
-        pltpu.make_async_copy(src.at[0], dst, sems.at[i])
-        for i, (src, dst) in enumerate(((q_hbm, q_ref), (k_hbm, k_ref), (v_hbm, v_ref)))
-    ]
+    pairs = (
+        (run_hbm, run_ref),
+        (freq_hbm, freq_ref),
+        (q_hbm.at[0], q_ref),
+        (k_hbm.at[0], k_ref),
+        (v_hbm.at[0], v_ref),
+    )
+    moves = [pltpu.make_async_copy(a, b, sems.at[i]) for i, (a, b) in enumerate(pairs)]
     for move in moves:
         move.start()
+    for move in moves[:2]:
+        move.wait()
     x_at, t_at = lax.axis_index("heads"), lax.axis_index("team")
     z_at, y_at = lax.axis_index("z"), lax.axis_index("yh") * YL + lax.axis_index("yl")
     run = run_ref[(t_at * Z + z_at) * Y + y_at]
@@ -65,7 +73,7 @@
         y = x * cosine + jnp.roll(x, HD // 2, axis=-1) * sine
         return jnp.swapaxes(y, 0, 1).astype(jnp.bfloat16)
 
-    for move in moves:
+    for move in moves[2:]:
         move.wait()
     n_g = k_ref.shape[1]
     o_ref[:, :Q_ROWS, :] = turned(q_ref).reshape(n_g, GROUP * PIECE, HD)
@@ -242,10 +250,11 @@
     packed = pl.pallas_call(
         pack_kernel,
         out_shape=jax.ShapeDtypeStruct((X * YL, (GROUP + 2) * PIECE, HD), bf),
-        in_specs=[smem, vmem, hbm, hbm, hbm],
+        in_specs=[hbm] * 5,
         out_specs=vmem,
-        scratch_shapes=[pltpu.VMEM(a.shape[1:], bf) for a in (queries, keys, values)]
-        + [pltpu.SemaphoreType.DMA((3,))],
+        scratch_shapes=[pltpu.SMEM((SLOTS,), jnp.int32), pltpu.VMEM((1, HD), jnp.float32)]
+        + [pltpu.VMEM(a.shape[1:], bf) for a in (queries, keys, values)]
+        + [pltpu.SemaphoreType.DMA((5,))],
         compiler_params=pltpu.CompilerParams(vmem_limit_bytes=60 << 20),
         name="pack",
     )(run_index, inverse_freqs(), queries, keys, values)

time: 98.2 us -> 97.5 us (level)
  no operation moved by 1% of the time
where the time goes in v6:
time: 97.5 us; the launch traced here: 97.2 us
  blocking collectives  69 us (71%)
  starting transfers between devices  14.3 us (15%)
  Pallas kernels  13.1 us (13%)
    all_gather x1, blocking collectives, per_device(): near = lax.all_gather(kv_own, 'z', axis=0, tiled=False)  32.4 us
    all_to_all x1, blocking collectives, per_device(): lax.all_to_all(partial.reshape(Y, MSG, LANES), ('yh', 'yl'), split_axis=0...  25 us
    all_to_all x1, blocking collectives, per_device(): lax.all_to_all(packed, ('heads', 'yl'), split_axis=0, concat_axis=0, tile...  11.7 us
    pallas_call x2, Pallas kernels, attend(): pl.pallas_call(functools.partial(attend_kernel, part), out_shape=out, in_...  9.6 us
    ppermute x1, starting transfers between devices, per_device(): far = lax.ppermute(near, 'team', [(0, 1), (1, 0)])  8.26 us
    all_to_all x1, starting transfers between devices, per_device(): q_all = lax.all_to_all(q_own, 'yh', split_axis=0, concat_axis=0, tiled=True)  6.02 us
  transfers between devices with their start and end apart: 2, of which 0 were waited for; matrix products, arithmetic and copies ran while one was open for 0% of the time, Pallas kernels for 5%

profile of v6, /device:TPU:1, one launch (start us, length us, event | category | flops | bytes accessed | tf_op | source)
XLA Modules:
  0.0 97.2 jit_solution(9000784161246958151)
XLA Ops:
  0.0 1.8 %pack.1 = bf16[8,96,128]{2,1,0:T(8,128)(2,1)} custom-call(s32[192]{0:T(256)} %run_ref.3, f32[1,128]{1,0:T(1,128)} %constant.2.clone.freq_hbm, bf16[1,16,32,128]{3,2,1,0:T(8,128)(2,1)} %q_hbm.1, bf16[1,16,8,128]{3,2,1,0:T(8,128)(2,1)} %k_hbm.1, bf16[1,16,8,128]{3,2,1,0:T(8,128)(2,1)} %v_hbm.1), custom_call_target="tpu_custom_call" | custom-call | tf_op jit(solution)/shard_map/pack/pallas_call | solution.py:250
  1.8 11.7 %all_to_all.15.mine_ref = bf16[8,96,128]{2,1,0:T(8,128)(2,1)S(1)} all-to-all(bf16[8,96,128]{2,1,0:T(8,128)(2,1)} %pack.1), channel_id=1, replica_groups=mesh['heads'=4,'team'=2,'z'=12,'yh'=4,'yl'=2] {'heads','yl'}, dimensions={0} | all-to-all | bytes 393216 | tf_op jit(solution)/shard_map/all_to_all | solution.py:261
  13.5 0.9 spread.1
  14.4 6.0 %all-to-all-start.1 = ((bf16[4,512,128]{2,1,0:T(8,128)(2,1)}), bf16[4,512,128]{2,1,0:T(8,128)(2,1)S(1)}, u32[]{:S(2)}, u32[]{:S(2)}) async-start(bf16[4,512,128]{2,1,0:T(8,128)(2,1)} %get-tuple-element.9), calls=%async_computation.1 | async-start | bytes 1048576 | tf_op jit(solution)/shard_map/all_to_all | solution.py:273
  20.4 32.4 %all-gather = bf16[3072,128]{1,0:T(8,128)(2,1)S(1)} all-gather(bf16[256,128]{1,0:T(8,128)(2,1)S(1)} %get-tuple-element.10), channel_id=2, replica_groups=mesh['heads'=4,'team'=2,'z'=12,'yh'=4,'yl'=2] {'z'}, dimensions={0}, use_global_device_ids=true | all-gather | bytes 851968 | tf_op jit(solution)/shard_map/all_gather | solution.py:274
  52.8 8.3 %collective-permute-start = (bf16[12,256,128]{2,1,0:T(8,128)(2,1)S(1)}, bf16[12,256,128]{2,1,0:T(8,128)(2,1)S(1)}, u32[]{:S(2)}, u32[]{:S(2)}) collective-permute-start(bf16[12,256,128]{2,1,0:T(8,128)(2,1)S(1)} %bitcast.8), channel_id=1, source_target_pairs={{0,96},{96,0},{1,97},{97,1},{2,98},{98,2},{3,99},{99,3},{4,100},{1... | collective-permute-start | bytes 2359304 | tf_op jit(solution)/shard_map/ppermute | solution.py:275
  61.0 0.0 all-to-all-done.1
  61.0 0.0 copy-start
  61.0 0.7 copy-done
  61.7 4.7 %attend_near.1 = (f32[4,2,128,256]{3,2,1,0:T(8,128)S(1)}, f32[4,2,8,256]{3,2,1,0:T(8,128)S(1)}) custom-call(s32[192]{0:T(256)S(1)} %copy-done, bf16[4,4,2,64,128]{4,3,2,1,0:T(8,128)(2,1)S(1)} %bitcast.6, bf16[12,4,2,2,16,128]{5,4,3,2,1,0:T(8,128)(2,1)S(1)} %bitcast.9), custom_call_target="tpu_custom_call" | custom-call | tf_op jit(solution)/shard_map/attend_near/pallas_call | solution.py:295
  66.4 0.0 collective-permute-done
  66.4 4.9 %attend_far.1 = bf16[4,2,264,128]{3,2,1,0:T(8,128)(2,1)S(1)} custom-call(s32[192]{0:T(256)S(1)} %copy-done, bf16[4,4,2,64,128]{4,3,2,1,0:T(8,128)(2,1)S(1)} %bitcast.7, bf16[12,4,2,2,16,128]{5,4,3,2,1,0:T(8,128)(2,1)S(1)} %bitcast.12, f32[4,2,128,256]{3,2,1,0:T(8,128)S(1)} %get-tuple-element.11.refs_0_, f32[4,2,8,256]{3,2,1,0:T(8,128)S(1)} %get-tuple-element.12.refs_1_), custom_call_target="tpu_custom_call" | custom-call | tf_op jit(solution)/shard_map/attend_far/pallas_call | solution.py:295
  71.3 25.0 %all_to_all.16 = bf16[8,264,128]{2,1,0:T(8,128)(2,1)S(1)} all-to-all(bf16[8,264,128]{2,1,0:T(8,128)(2,1)S(1)} %bitcast.10), channel_id=1, replica_groups=mesh['heads'=4,'team'=2,'z'=12,'yh'=4,'yl'=2] {'yh','yl'}, dimensions={0} | all-to-all | bytes 1081344 | tf_op jit(solution)/shard_map/all_to_all | solution.py:306
  96.3 0.9 combine.1
Async XLA Ops:
  14.4 46.7 %all-to-all-start.1 = ((bf16[4,512,128]{2,1,0:T(8,128)(2,1)}), bf16[4,512,128]{2,1,0:T(8,128)(2,1)S(1)}, u32[]{:S(2)}, u32[]{:S(2)}) async-start(bf16[4,512,128]{2,1,0:T(8,128)(2,1)} %get-tuple-element.9), calls=%async_computation.1 | async-start | bytes 1048576 | tf_op jit(solution)/shard_map/all_to_all | solution.py:273
  52.8 13.7 %collective-permute-start = (bf16[12,256,128]{2,1,0:T(8,128)(2,1)S(1)}, bf16[12,256,128]{2,1,0:T(8,128)(2,1)S(1)}, u32[]{:S(2)}, u32[]{:S(2)}) collective-permute-start(bf16[12,256,128]{2,1,0:T(8,128)(2,1)S(1)} %bitcast.8), channel_id=1, source_target_pairs={{0,96},{96,0},{1,97},{97,1},{2,98},{98,2},{3,99},{99,3},{4,100},{1... | collective-permute-start | bytes 2359304 | tf_op jit(solution)/shard_map/ppermute | solution.py:275
  61.0 0.7 copy-start

commit v7 on v6

--- a/solution.py
+++ b/solution.py
@@ -89,8 +89,11 @@
     kv_ref[...] = mine_ref[:, Q_ROWS:, :].reshape(X * YL * 2 * PIECE, HD)
 
 
-def attend_kernel(part, run_ref, q_ref, kv_ref, *refs):
+def attend_kernel(part, run_hbm, q_ref, kv_ref, *refs):
     bf, f32 = jnp.bfloat16, jnp.float32
+    *refs, run_ref, sem = refs
+    fetch = pltpu.make_async_copy(run_hbm, run_ref, sem)
+    fetch.start()
     if part == 0:
         acc_ref, st_ref, k_s, vt_s, se_s, sl_s, w_s, own_s = refs
     else:
@@ -106,6 +109,7 @@
         rows = slice(half * PART, (half + 1) * PART)
         k_s[rows, :HD] = picked[:, :, :, 0].reshape(PART, HD)
         vt_s[:, rows] = picked[:, :, :, 1].reshape(PART, HD).T
+    fetch.wait()
     for z in range(Z):
         for yl in range(YL):
             slot = z * YL + yl
@@ -242,9 +246,12 @@
             o_ref[at : at + PIECE] = jnp.swapaxes(block, 0, 1).astype(jnp.bfloat16)
 
 
+def in_hbm(value):
+    return pltpu.with_memory_space_constraint(value, pltpu.HBM)
+
+
 def per_device(queries, keys, values, run_index):
     bf, f32 = jnp.bfloat16, jnp.float32
-    smem = pl.BlockSpec(memory_space=pltpu.SMEM)
     vmem = pl.BlockSpec(memory_space=pltpu.VMEM)
     hbm = pl.BlockSpec(memory_space=pltpu.HBM)
     packed = pl.pallas_call(
@@ -255,9 +262,9 @@
         scratch_shapes=[pltpu.SMEM((SLOTS,), jnp.int32), pltpu.VMEM((1, HD), jnp.float32)]
         + [pltpu.VMEM(a.shape[1:], bf) for a in (queries, keys, values)]
         + [pltpu.SemaphoreType.DMA((5,))],
-        compiler_params=pltpu.CompilerParams(vmem_limit_bytes=60 << 20),
+        compiler_params=pltpu.CompilerParams(vmem_limit_bytes=8 << 20),
         name="pack",
-    )(run_index, inverse_freqs(), queries, keys, values)
+    )(*map(in_hbm, (run_index, jnp.asarray(inverse_freqs()), queries, keys, values)))
     mine = lax.all_to_all(packed, ("heads", "yl"), split_axis=0, concat_axis=0, tiled=True)
     q_own, kv_own = pl.pallas_call(
         spread_kernel,
@@ -295,12 +302,14 @@
         return pl.pallas_call(
             functools.partial(attend_kernel, part),
             out_shape=out,
-            in_specs=[smem, vmem, vmem] + [vmem] * len(state),
+            in_specs=[hbm, vmem, vmem] + [vmem] * len(state),
             out_specs=(vmem, vmem) if part == 0 else vmem,
-            scratch_shapes=scratch + [pltpu.VMEM((YL, LANES, HD), f32)] * (part == 0),
+            scratch_shapes=scratch
+            + [pltpu.VMEM((YL, LANES, HD), f32)] * (part == 0)
+            + [pltpu.SMEM((SLOTS,), jnp.int32), pltpu.SemaphoreType.DMA],
             compiler_params=pltpu.CompilerParams(vmem_limit_bytes=20 << 20),
             name=("attend_near", "attend_far")[part],
-        )(run_index, q_all, kv.reshape(kv_shape), *state)
+        )(in_hbm(run_index), q_all, kv.reshape(kv_shape), *state)
 
     partial = attend(1, far, *attend(0, near))
     parts = lax.all_to_all(

time: 97.5 us -> 96.1 us (0.986)
  no operation moved by 1% of the time
where the time goes in v7:
time: 96.1 us; the launch traced here: 95.8 us
  blocking collectives  68.6 us (71%)
  starting transfers between devices  14.5 us (15%)
  Pallas kernels  12.7 us (13%)
    all_gather x1, blocking collectives, per_device(): near = lax.all_gather(kv_own, 'z', axis=0, tiled=False)  32.4 us
    all_to_all x1, blocking collectives, per_device(): lax.all_to_all(partial.reshape(Y, MSG, LANES), ('yh', 'yl'), split_axis=0...  24.8 us
    all_to_all x1, blocking collectives, per_device(): lax.all_to_all(packed, ('heads', 'yl'), split_axis=0, concat_axis=0, tile...  11.5 us
    pallas_call x2, Pallas kernels, attend(): pl.pallas_call(functools.partial(attend_kernel, part), out_shape=out, in_...  9.79 us
    ppermute x1, starting transfers between devices, per_device(): far = lax.ppermute(near, 'team', [(0, 1), (1, 0)])  8.44 us
    all_to_all x1, starting transfers between devices, per_device(): q_all = lax.all_to_all(q_own, 'yh', split_axis=0, concat_axis=0, tiled=True)  6.02 us
  transfers between devices with their start and end apart: 2, of which 0 were waited for; matrix products, arithmetic and copies ran while one was open for 0% of the time, Pallas kernels for 5%

profile of v7, /device:TPU:1, one launch (start us, length us, event | category | flops | bytes accessed | tf_op | source)
XLA Modules:
  0.0 95.8 jit_solution(450690606190540555)
XLA Ops:
  0.0 1.1 %pack.1 = bf16[8,96,128]{2,1,0:T(8,128)(2,1)S(1)} custom-call(s32[192]{0:T(256)} %run_hbm.5, f32[1,128]{1,0:T(1,128)} %constant.2.clone.freq_hbm, bf16[1,16,32,128]{3,2,1,0:T(8,128)(2,1)} %q_hbm.1, bf16[1,16,8,128]{3,2,1,0:T(8,128)(2,1)} %k_hbm.1, bf16[1,16,8,128]{3,2,1,0:T(8,128)(2,1)} %v_hbm.1), custom_call_target="tpu_custom_call" | custom-call | tf_op jit(solution)/shard_map/pack/pallas_call | solution.py:257
  1.2 11.5 %all_to_all.15.mine_ref = bf16[8,96,128]{2,1,0:T(8,128)(2,1)S(1)} all-to-all(bf16[8,96,128]{2,1,0:T(8,128)(2,1)S(1)} %pack.1), channel_id=1, replica_groups=mesh['heads'=4,'team'=2,'z'=12,'yh'=4,'yl'=2] {'heads','yl'}, dimensions={0} | all-to-all | bytes 393216 | tf_op jit(solution)/shard_map/all_to_all | solution.py:268
  12.6 0.9 spread.1
  13.5 6.0 %all-to-all-start.1 = ((bf16[4,512,128]{2,1,0:T(8,128)(2,1)}), bf16[4,512,128]{2,1,0:T(8,128)(2,1)S(1)}, u32[]{:S(2)}, u32[]{:S(2)}) async-start(bf16[4,512,128]{2,1,0:T(8,128)(2,1)} %get-tuple-element.9), calls=%async_computation.1 | async-start | bytes 1048576 | tf_op jit(solution)/shard_map/all_to_all | solution.py:280
  19.5 32.4 %all-gather = bf16[3072,128]{1,0:T(8,128)(2,1)S(1)} all-gather(bf16[256,128]{1,0:T(8,128)(2,1)S(1)} %get-tuple-element.10), channel_id=2, replica_groups=mesh['heads'=4,'team'=2,'z'=12,'yh'=4,'yl'=2] {'z'}, dimensions={0}, use_global_device_ids=true | all-gather | bytes 851968 | tf_op jit(solution)/shard_map/all_gather | solution.py:281
  51.9 8.4 %collective-permute-start = (bf16[12,256,128]{2,1,0:T(8,128)(2,1)S(1)}, bf16[12,256,128]{2,1,0:T(8,128)(2,1)S(1)}, u32[]{:S(2)}, u32[]{:S(2)}) collective-permute-start(bf16[12,256,128]{2,1,0:T(8,128)(2,1)S(1)} %bitcast.8), channel_id=1, source_target_pairs={{0,96},{96,0},{1,97},{97,1},{2,98},{98,2},{3,99},{99,3},{4,100},{1... | collective-permute-start | bytes 2359304 | tf_op jit(solution)/shard_map/ppermute | solution.py:282
  60.3 0.0 all-to-all-done.1
  60.3 4.8 %attend_near.1 = (f32[4,2,128,256]{3,2,1,0:T(8,128)S(1)}, f32[4,2,8,256]{3,2,1,0:T(8,128)S(1)}) custom-call(s32[192]{0:T(256)} %run_hbm.5, bf16[4,4,2,64,128]{4,3,2,1,0:T(8,128)(2,1)S(1)} %bitcast.6, bf16[12,4,2,2,16,128]{5,4,3,2,1,0:T(8,128)(2,1)S(1)} %bitcast.9), custom_call_target="tpu_custom_call" | custom-call | tf_op jit(solution)/shard_map/attend_near/pallas_call | solution.py:302
  65.1 0.0 collective-permute-done
  65.1 5.0 %attend_far.1 = bf16[4,2,264,128]{3,2,1,0:T(8,128)(2,1)S(1)} custom-call(s32[192]{0:T(256)} %run_hbm.5, bf16[4,4,2,64,128]{4,3,2,1,0:T(8,128)(2,1)S(1)} %bitcast.7, bf16[12,4,2,2,16,128]{5,4,3,2,1,0:T(8,128)(2,1)S(1)} %bitcast.12, f32[4,2,128,256]{3,2,1,0:T(8,128)S(1)} %get-tuple-element.11.refs_0_, f32[4,2,8,256]{3,2,1,0:T(8,128)S(1)} %get-tuple-element.12.refs_1_), custom_call_target="tpu_custom_call" | custom-call | tf_op jit(solution)/shard_map/attend_far/pallas_call | solution.py:302
  70.2 24.8 %all_to_all.16 = bf16[8,264,128]{2,1,0:T(8,128)(2,1)S(1)} all-to-all(bf16[8,264,128]{2,1,0:T(8,128)(2,1)S(1)} %bitcast.10), channel_id=1, replica_groups=mesh['heads'=4,'team'=2,'z'=12,'yh'=4,'yl'=2] {'yh','yl'}, dimensions={0} | all-to-all | bytes 1081344 | tf_op jit(solution)/shard_map/all_to_all | solution.py:315
  95.0 0.9 combine.1
Async XLA Ops:
  13.5 46.8 %all-to-all-start.1 = ((bf16[4,512,128]{2,1,0:T(8,128)(2,1)}), bf16[4,512,128]{2,1,0:T(8,128)(2,1)S(1)}, u32[]{:S(2)}, u32[]{:S(2)}) async-start(bf16[4,512,128]{2,1,0:T(8,128)(2,1)} %get-tuple-element.9), calls=%async_computation.1 | async-start | bytes 1048576 | tf_op jit(solution)/shard_map/all_to_all | solution.py:280
  51.9 13.3 %collective-permute-start = (bf16[12,256,128]{2,1,0:T(8,128)(2,1)S(1)}, bf16[12,256,128]{2,1,0:T(8,128)(2,1)S(1)}, u32[]{:S(2)}, u32[]{:S(2)}) collective-permute-start(bf16[12,256,128]{2,1,0:T(8,128)(2,1)S(1)} %bitcast.8), channel_id=1, source_target_pairs={{0,96},{96,0},{1,97},{97,1},{2,98},{98,2},{3,99},{99,3},{4,100},{1... | collective-permute-start | bytes 2359304 | tf_op jit(solution)/shard_map/ppermute | solution.py:282

commit v8 on v7

--- a/solution.py
+++ b/solution.py
@@ -82,11 +82,16 @@
     o_ref[:, Q_ROWS + PIECE :, :] = v
 
 
-def spread_kernel(mine_ref, q_ref, kv_ref):
-    q = mine_ref[:, :Q_ROWS, :].reshape(X * YL * Q_ROWS, HD)
-    for i in range(YH):
-        q_ref[i] = q
+def spread_kernel(mine_ref, q_hbm, kv_ref, sems):
+    moves = [
+        pltpu.make_async_copy(mine_ref.at[:, :Q_ROWS, :], q_hbm.at[i], sems.at[i])
+        for i in range(YH)
+    ]
+    for move in moves:
+        move.start()
     kv_ref[...] = mine_ref[:, Q_ROWS:, :].reshape(X * YL * 2 * PIECE, HD)
+    for move in moves:
+        move.wait()
 
 
 def attend_kernel(part, run_hbm, q_ref, kv_ref, *refs):
@@ -269,11 +274,12 @@
     q_own, kv_own = pl.pallas_call(
         spread_kernel,
         out_shape=(
-            jax.ShapeDtypeStruct((YH, X * YL * Q_ROWS, HD), bf),
+            jax.ShapeDtypeStruct((YH, X * YL, Q_ROWS, HD), bf),
             jax.ShapeDtypeStruct((X * YL * 2 * PIECE, HD), bf),
         ),
         in_specs=[vmem],
-        out_specs=(vmem, vmem),
+        out_specs=(hbm, vmem),
+        scratch_shapes=[pltpu.SemaphoreType.DMA((YH,))],
         compiler_params=pltpu.CompilerParams(vmem_limit_bytes=8 << 20),
         name="spread",
     )(mine)

time: 96.1 us -> 96.1 us (level)
  no operation moved by 1% of the time
where the time goes in v8:
time: 96.1 us; the launch traced here: 95.8 us
  blocking collectives  68.6 us (71%)
  starting transfers between devices  14.5 us (15%)
  Pallas kernels  12.6 us (13%)
    all_gather x1, blocking collectives, per_device(): near = lax.all_gather(kv_own, 'z', axis=0, tiled=False)  32.4 us
    all_to_all x1, blocking collectives, per_device(): lax.all_to_all(partial.reshape(Y, MSG, LANES), ('yh', 'yl'), split_axis=0...  24.8 us
    all_to_all x1, blocking collectives, per_device(): lax.all_to_all(packed, ('heads', 'yl'), split_axis=0, concat_axis=0, tile...  11.5 us
    pallas_call x2, Pallas kernels, attend(): pl.pallas_call(functools.partial(attend_kernel, part), out_shape=out, in_...  9.79 us
    ppermute x1, starting transfers between devices, per_device(): far = lax.ppermute(near, 'team', [(0, 1), (1, 0)])  8.44 us
    all_to_all x1, starting transfers between devices, per_device(): q_all = lax.all_to_all(q_own, 'yh', split_axis=0, concat_axis=0, tiled=True)  6.03 us
  transfers between devices with their start and end apart: 2, of which 0 were waited for; matrix products, arithmetic and copies ran while one was open for 0% of the time, Pallas kernels for 5%

profile of v8, /device:TPU:1, one launch (start us, length us, event | category | flops | bytes accessed | tf_op | source)
XLA Modules:
  0.0 95.8 jit_solution(7490012400562122898)
XLA Ops:
  0.0 1.1 %pack.1 = bf16[8,96,128]{2,1,0:T(8,128)(2,1)S(1)} custom-call(s32[192]{0:T(256)} %run_hbm.5, f32[1,128]{1,0:T(1,128)} %constant.2.clone.freq_hbm, bf16[1,16,32,128]{3,2,1,0:T(8,128)(2,1)} %q_hbm.1, bf16[1,16,8,128]{3,2,1,0:T(8,128)(2,1)} %k_hbm.1, bf16[1,16,8,128]{3,2,1,0:T(8,128)(2,1)} %v_hbm.1), custom_call_target="tpu_custom_call" | custom-call | tf_op jit(solution)/shard_map/pack/pallas_call | solution.py:262
  1.2 11.5 %all_to_all.15.mine_ref = bf16[8,96,128]{2,1,0:T(8,128)(2,1)S(1)} all-to-all(bf16[8,96,128]{2,1,0:T(8,128)(2,1)S(1)} %pack.1), channel_id=1, replica_groups=mesh['heads'=4,'team'=2,'z'=12,'yh'=4,'yl'=2] {'heads','yl'}, dimensions={0} | all-to-all | bytes 393216 | tf_op jit(solution)/shard_map/all_to_all | solution.py:273
  12.6 0.8 spread.1
  13.5 6.0 %all-to-all-start.1 = ((bf16[4,8,64,128]{3,2,1,0:T(8,128)(2,1)}), bf16[4,8,64,128]{3,2,1,0:T(8,128)(2,1)S(1)}, u32[]{:S(2)}, u32[]{:S(2)}) async-start(bf16[4,8,64,128]{3,2,1,0:T(8,128)(2,1)} %get-tuple-element.9), calls=%async_computation.1 | async-start | bytes 1048576 | tf_op jit(solution)/shard_map/all_to_all | solution.py:286
  19.5 32.4 %all-gather = bf16[3072,128]{1,0:T(8,128)(2,1)S(1)} all-gather(bf16[256,128]{1,0:T(8,128)(2,1)S(1)} %get-tuple-element.10), channel_id=2, replica_groups=mesh['heads'=4,'team'=2,'z'=12,'yh'=4,'yl'=2] {'z'}, dimensions={0}, use_global_device_ids=true | all-gather | bytes 851968 | tf_op jit(solution)/shard_map/all_gather | solution.py:287
  51.9 8.4 %collective-permute-start = (bf16[12,256,128]{2,1,0:T(8,128)(2,1)S(1)}, bf16[12,256,128]{2,1,0:T(8,128)(2,1)S(1)}, u32[]{:S(2)}, u32[]{:S(2)}) collective-permute-start(bf16[12,256,128]{2,1,0:T(8,128)(2,1)S(1)} %bitcast.8), channel_id=1, source_target_pairs={{0,96},{96,0},{1,97},{97,1},{2,98},{98,2},{3,99},{99,3},{4,100},{1... | collective-permute-start | bytes 2359304 | tf_op jit(solution)/shard_map/ppermute | solution.py:288
  60.3 0.0 all-to-all-done.1
  60.3 4.8 %attend_near.1 = (f32[4,2,128,256]{3,2,1,0:T(8,128)S(1)}, f32[4,2,8,256]{3,2,1,0:T(8,128)S(1)}) custom-call(s32[192]{0:T(256)} %run_hbm.5, bf16[4,4,2,64,128]{4,3,2,1,0:T(8,128)(2,1)S(1)} %bitcast.6, bf16[12,4,2,2,16,128]{5,4,3,2,1,0:T(8,128)(2,1)S(1)} %bitcast.9), custom_call_target="tpu_custom_call" | custom-call | tf_op jit(solution)/shard_map/attend_near/pallas_call | solution.py:308
  65.1 0.0 collective-permute-done
  65.1 5.0 %attend_far.1 = bf16[4,2,264,128]{3,2,1,0:T(8,128)(2,1)S(1)} custom-call(s32[192]{0:T(256)} %run_hbm.5, bf16[4,4,2,64,128]{4,3,2,1,0:T(8,128)(2,1)S(1)} %bitcast.7, bf16[12,4,2,2,16,128]{5,4,3,2,1,0:T(8,128)(2,1)S(1)} %bitcast.12, f32[4,2,128,256]{3,2,1,0:T(8,128)S(1)} %get-tuple-element.11.refs_0_, f32[4,2,8,256]{3,2,1,0:T(8,128)S(1)} %get-tuple-element.12.refs_1_), custom_call_target="tpu_custom_call" | custom-call | tf_op jit(solution)/shard_map/attend_far/pallas_call | solution.py:308
  70.1 24.8 %all_to_all.16 = bf16[8,264,128]{2,1,0:T(8,128)(2,1)S(1)} all-to-all(bf16[8,264,128]{2,1,0:T(8,128)(2,1)S(1)} %bitcast.10), channel_id=1, replica_groups=mesh['heads'=4,'team'=2,'z'=12,'yh'=4,'yl'=2] {'yh','yl'}, dimensions={0} | all-to-all | bytes 1081344 | tf_op jit(solution)/shard_map/all_to_all | solution.py:321
  94.9 0.9 combine.1
Async XLA Ops:
  13.5 46.9 %all-to-all-start.1 = ((bf16[4,8,64,128]{3,2,1,0:T(8,128)(2,1)}), bf16[4,8,64,128]{3,2,1,0:T(8,128)(2,1)S(1)}, u32[]{:S(2)}, u32[]{:S(2)}) async-start(bf16[4,8,64,128]{3,2,1,0:T(8,128)(2,1)} %get-tuple-element.9), calls=%async_computation.1 | async-start | bytes 1048576 | tf_op jit(solution)/shard_map/all_to_all | solution.py:286
  51.9 13.3 %collective-permute-start = (bf16[12,256,128]{2,1,0:T(8,128)(2,1)S(1)}, bf16[12,256,128]{2,1,0:T(8,128)(2,1)S(1)}, u32[]{:S(2)}, u32[]{:S(2)}) collective-permute-start(bf16[12,256,128]{2,1,0:T(8,128)(2,1)S(1)} %bitcast.8), channel_id=1, source_target_pairs={{0,96},{96,0},{1,97},{97,1},{2,98},{98,2},{3,99},{99,3},{4,100},{1... | collective-permute-start | bytes 2359304 | tf_op jit(solution)/shard_map/ppermute | solution.py:288
